TPU v7x, 32 devices: a whole 2x2x4 slice. The times are simulated.
32 devices in a mesh: groups: 2 (over x), panel: 16 (over z, y, core).
Axes of the slice: x: 2, y: 2, z: 4, core: 2. Of those that a mesh axis runs over, the one named last changes fastest.
Arguments:
- eig_vectors: bfloat16 [5120, 1024], P(('groups', 'panel')), parts along dimension 0, may hold values from -0.1875 to 0.1875
- eig_values: bfloat16 [5120], P(('groups', 'panel')), parts along dimension 0, may hold values from 0.19921875 to 5
- eig_count: int32 [16], P('groups'), parts along dimension 0, may hold values from 128 to 512, as said below
- snp_count: int32 [16], P('groups'), parts along dimension 0, may hold values from 512 to 1024
- zscores: bfloat16 [32, 8, 1024, 128], P(('groups', 'panel')), parts along dimension 0, may hold values from -6 to 6
- samples: bfloat16 [4096], P('groups'), parts along dimension 0, may hold values from 20 to 160
Outputs:
- covariance: float32 [9, 32, 8, 128, 128], P(None, ('groups', 'panel')), parts along dimension 1
There are 2 independent parts, one for each index of `groups`. A program takes and returns all parts, laid end to end along the dimension named above; each array names one. Nothing has to cross between parts.
Inputs may be any that keep to these rules, and one draw needn't show every extreme that they name: `eig_count`: blocks 2m and 2m+1 hold 640 eigenvectors together, so every block group holds 2560; some block holds exactly 512.
All inputs are finite; a program needn't handle non-finite values.
Results may differ from a plain program's by a relative error of at most 0.0045.
Values may be sent and summed in bfloat16 or wider, within the bound.
A program may use at most 64 MiB of HBM per device.

v0:
```python
import functools

import jax
import jax.numpy as jnp
from jax import lax
from jax.experimental import pallas as pl
from jax.experimental.pallas import tpu as pltpu
from jax.sharding import PartitionSpec as P

ROUNDS = 8
LIMIT = 56 * 1024 * 1024


def place_masked(snps, scores, pair, store):
    width = scores.shape[-1]
    for side in range(2):
        block = 2 * pair + side
        rows = lax.broadcasted_iota(jnp.int32, scores.shape[-2:], 0)
        part = jnp.where(rows < snps[block], scores[side].astype(jnp.float32), 0.0)
        store[:, side * width : (side + 1) * width] = part.astype(jnp.bfloat16)


def project_rows(vectors, masked, first_count):
    both = jnp.dot(vectors, masked, preferred_element_type=jnp.float32)
    width = both.shape[1] // 2
    rows = lax.broadcasted_iota(jnp.int32, (both.shape[0], width), 0)
    return jnp.where(rows < first_count, both[:, :width], both[:, width:]).astype(jnp.bfloat16)


def project_kernel(counts, snps, vectors, scores, out, masked):
    pair = pl.program_id(0)
    place_masked(snps, scores.at[0], pair, masked)
    out[...] = project_rows(vectors[...], masked[...], counts[2 * pair])


def project(vectors, scores, counts, snps):
    row_total, depth = vectors.shape
    blocks, snp_rows, width = scores.shape[1:]
    pair_rows = 2 * row_total // blocks
    return pl.pallas_call(
        project_kernel,
        out_shape=jax.ShapeDtypeStruct((row_total, width), jnp.bfloat16),
        grid_spec=pltpu.PrefetchScalarGridSpec(
            num_scalar_prefetch=2,
            grid=(blocks // 2,),
            in_specs=[
                pl.BlockSpec((pair_rows, depth), lambda b, *_: (b, 0)),
                pl.BlockSpec((1, 2, snp_rows, width), lambda b, *_: (0, b, 0, 0)),
            ],
            out_specs=pl.BlockSpec((pair_rows, width), lambda b, *_: (b, 0)),
            scratch_shapes=[pltpu.VMEM((snp_rows, 2 * width), jnp.bfloat16)],
        ),
        compiler_params=pltpu.CompilerParams(vmem_limit_bytes=LIMIT),
    )(counts, snps, vectors, scores)


def gram_kernel(counts, slots, weighted, panels, scale, out):
    pair = pl.program_id(0)
    width = weighted.shape[1]
    left = weighted[...].astype(jnp.float32)
    rows = lax.broadcasted_iota(jnp.int32, left.shape, 0)
    first = rows < counts[2 * pair]
    left = jnp.concatenate([jnp.where(first, left, 0.0).T, jnp.where(first, 0.0, left).T], axis=0)
    left = left.astype(jnp.bfloat16)
    shape = (width, width)
    same = lax.broadcasted_iota(jnp.int32, shape, 0) == lax.broadcasted_iota(jnp.int32, shape, 1)
    for index in range(out.shape[0]):
        both = jnp.dot(left, panels[slots[index]], preferred_element_type=jnp.float32)
        for side in range(2):
            gram = both[side * width : (side + 1) * width]
            if index == 0:
                count = counts[2 * pair + side].astype(jnp.float32)
                gram = gram - jnp.where(same, count, 0.0)
            out[index, 0, side] = gram * scale[index]


def grams(weighted, panels, scale, slots, counts):
    blocks = counts.shape[0]
    rounds, width = scale.shape[:2]
    pair_rows = 2 * weighted.shape[0] // blocks
    return pl.pallas_call(
        gram_kernel,
        out_shape=jax.ShapeDtypeStruct((rounds, 1, blocks, width, width), jnp.float32),
        grid_spec=pltpu.PrefetchScalarGridSpec(
            num_scalar_prefetch=2,
            grid=(blocks // 2,),
            in_specs=[
                pl.BlockSpec((pair_rows, width), lambda b, *_: (b, 0)),
                pl.BlockSpec((panels.shape[0], pair_rows, width), lambda b, *_: (0, b, 0)),
                pl.BlockSpec(scale.shape, lambda b, *_: (0, 0, 0)),
            ],
            out_specs=pl.BlockSpec((rounds, 1, 2, width, width), lambda b, *_: (0, 0, b, 0, 0)),
        ),
        compiler_params=pltpu.CompilerParams(vmem_limit_bytes=LIMIT),
    )(counts, slots, weighted, panels, scale)


def exchange_kernel(counts, snps, own, own_values, scores, out, held, values, left, store, masked,
                    here, send1, recv1, send2, recv2, send3, recv3):
    line = lax.axis_size("panel") // 4
    me = lax.axis_index("panel")
    z = me // 4
    y = (me // 2) % 2
    k = me % 2
    piece = own.shape[0]
    pair_rows = 4 * piece
    halves = recv1.shape[1]
    part = piece // halves
    chunks = recv2.shape[1]
    top = line - 1
    up, down, across, beside = me + 4, me - 4, me + 2 - 4 * y, me + 1 - 2 * k
    pending = []

    barrier = pltpu.get_barrier_semaphore()
    others = 4 * line - 1
    for step in range(1, others + 1):
        target = lax.rem(me + step, others + 1)
        pl.semaphore_signal(
            barrier, inc=1, device_id={"panel": target}, device_id_type=pl.DeviceIdType.MESH
        )
    pl.semaphore_wait(barrier, others)

    def start(condition, copy):
        if condition is None:
            copy.start()
        else:
            pl.when(condition)(copy.start)
        pending.append((condition, copy))

    def move1(source, half, way, target, first=False):
        rows = pl.ds(source * piece + half * part, part)
        origin = own.at[pl.ds(half * part, part)] if first else store.at[rows]
        return pltpu.make_async_remote_copy(
            src_ref=origin,
            dst_ref=store.at[rows],
            send_sem=send1.at[way, source, half],
            recv_sem=recv1.at[source, half],
            device_id={"panel": target},
            device_id_type=pl.DeviceIdType.MESH,
        )

    def arrive1(source, half):
        move1(source, half, 0, beside).wait_recv()

    def move2(source, chunk, way, target):
        rows = pl.ds(chunk * pair_rows, pair_rows)
        return pltpu.make_async_remote_copy(
            src_ref=held.at[source, rows],
            dst_ref=held.at[source, rows],
            send_sem=send2.at[way, source, chunk],
            recv_sem=recv2.at[source, chunk],
            device_id={"panel": target},
            device_id_type=pl.DeviceIdType.MESH,
        )

    def arrive2(source, chunk):
        move2(source, chunk, 0, beside).wait_recv()

    def move3(source, step, target):
        return pltpu.make_async_remote_copy(
            src_ref=own_values,
            dst_ref=values.at[source],
            send_sem=send3.at[step],
            recv_sem=recv3.at[source],
            device_id={"panel": target},
            device_id_type=pl.DeviceIdType.MESH,
        )

    def spread(condition, chunk, source, behind):
        side = (behind >= y) & (behind <= y + 1)
        near = behind <= 2
        start(condition & side, move2(source, chunk, 2, across))
        start(condition & near, move2(source, chunk, 3, beside))

    def order(source, step):
        far = source // 4
        near = jnp.minimum(far, top - far)
        nearest = jnp.where(step > 2 * near, step, (near + (step + 1) // 2 * (1 - 2 * (step % 2))))
        return jnp.where(far > top - far, top - nearest, nearest)

    for half in range(halves):
        start(z < top, move1(me, half, 0, up, True))
        start(z > 0, move1(me, half, 1, down, True))
        start(None, move1(me, half, 2, across, True))
        start(None, move1(me, half, 3, beside, True))
    for step in range(1, others + 1):
        start(None, move3(me, step, lax.rem(me + step, others + 1)))
    local = [
        pltpu.make_async_copy(own, store.at[pl.ds(me * piece, piece)], here.at[0]),
        pltpu.make_async_copy(own_values, values.at[me], here.at[1]),
    ]
    for copy in local:
        copy.start()
    for pair in range(line):
        place_masked(snps, scores.at[0, pl.ds(2 * pair, 2)], pair, masked.at[pair])
    for copy in local:
        copy.wait()

    def plane(index):
        rows = pl.ds(index * pair_rows, pair_rows)
        held[me, rows] = project_rows(store[rows], masked[index], counts[2 * index])

    def column(distance):
        for half in range(halves):
            def below():
                arrive1(me - 4 * distance, half)
            def above():
                arrive1(me + 4 * distance, half)
            has_below, has_above = z >= distance, z + distance <= top
            pl.when(has_below)(below)
            source = me - 4 * distance
            start(has_below & (z < top), move1(source, half, 0, up))
            start(has_below, move1(source, half, 2, across))
            start(has_below, move1(source, half, 3, beside))
            pl.when(has_above)(above)
            source = me + 4 * distance
            start(has_above & (z > 0), move1(source, half, 1, down))
            start(has_above, move1(source, half, 2, across))
            start(has_above, move1(source, half, 3, beside))

    def sideways(distance, sign):
        has = (z >= distance) if sign < 0 else (z + distance <= top)
        source = across + sign * 4 * distance
        for half in range(halves):
            pl.when(has)(functools.partial(arrive1, source, half))
            start(has, move1(source, half, 3, beside))

    def finish(distance, sign):
        has = (z >= distance) if sign < 0 else (z + distance <= top)

        @pl.when(has)
        def _():
            for source in (beside, beside + 2 - 4 * y):
                for half in range(halves):
                    arrive1(source + sign * 4 * distance, half)
            plane(z + sign * distance)

        chunk = z + sign * distance
        start(has & (z < top), move2(me, chunk, 0, up))
        start(has & (z >= line - 2), move2(me, chunk, 1, down))
        spread(has, chunk, me, 0)

    for distance in range(1, line + 1):
        if distance < line:
            column(distance)
        last = distance - 1
        signs = (1,) if last == 0 else (-1, 1)
        for sign in signs:
            sideways(last, sign)
        for sign in signs:
            finish(last, sign)

    cross = []
    for lag in range(2):
        plane_index = lax.rem(z - lag - (1 - y) + line, line)
        cross.append(plane_index * 4 + (1 - y) * 2 + k)
    def weigh(index):
        rows = pl.ds(index * pair_rows, pair_rows)
        row = values[4 * index] + values[4 * index + 1]
        row = row + (values[4 * index + 2] + values[4 * index + 3])
        flat = held[me, rows].astype(jnp.float32).T / row[0:1]
        first = lax.broadcasted_iota(jnp.int32, flat.shape, 1) < counts[2 * index]
        both = jnp.concatenate([jnp.where(first, flat, 0.0), jnp.where(first, 0.0, flat)], axis=0)
        left[index] = both.astype(jnp.bfloat16)

    def gram(source, chunk, number, own_panel=False):
        rows = pl.ds(chunk * pair_rows, pair_rows)
        both = jnp.dot(left[chunk], held[source, rows], preferred_element_type=jnp.float32)
        width = both.shape[1]
        for side in range(2):
            part = both[side * width : (side + 1) * width]
            if own_panel:
                shape = (width, width)
                across_rows = lax.broadcasted_iota(jnp.int32, shape, 0)
                same = across_rows == lax.broadcasted_iota(jnp.int32, shape, 1)
                count = counts[2 * chunk + side].astype(jnp.float32)
                part = part - jnp.where(same, count, 0.0)
            out[number, 0, 2 * chunk + side] = part

    near = [lax.rem(z - lag + line, line) * 4 + y * 2 + k for lag in range(3)]
    swap = 1 - 2 * k

    for step in range(chunks + 2):
        if step < chunks:
            for distance in range(1, line):
                if distance <= 2:
                    has = z >= distance
                    source = me - 4 * distance
                    chunk = order(source, step)
                    pl.when(has)(functools.partial(arrive2, source, chunk))
                    if distance == 1:
                        start(has & (z < top), move2(source, chunk, 0, up))
                    spread(has, chunk, source, distance)
                has = (z + distance <= top) & (z + distance >= line - 2)
                source = me + 4 * distance
                chunk = order(source, step)
                pl.when(has)(functools.partial(arrive2, source, chunk))
                start(has & (z > 0), move2(source, chunk, 1, down))
                spread(has, chunk, source, line - distance)
        if step == 0:
            for number in range(1, others + 1):
                move3(lax.rem(me + number, others + 1), number, beside).wait_recv()
            for index in range(chunks):
                weigh(index)
        if 0 < step <= chunks:
            for source in cross:
                chunk = order(source, step - 1)
                arrive2(source, chunk)
                start(None, move2(source, chunk, 3, beside))
        if 0 < step <= chunks:
            for lag, source in enumerate(near):
                gram(source, order(source, step - 1), 4 * lag, lag == 0)
            for lag, source in enumerate(cross):
                gram(source, order(source, step - 1), 4 * lag + 2)
        if step > 1:
            for lag, source in enumerate(near):
                chunk = order(source, step - 2)
                arrive2(source + swap, chunk)
                number = 4 * lag - swap

                @pl.when((number >= 0) & (number < out.shape[0]))
                def _():
                    gram(source + swap, chunk, number)

            for lag, source in enumerate(cross):
                chunk = order(source, step - 2)
                arrive2(source + swap, chunk)
                gram(source + swap, chunk, 4 * lag + 2 - swap)
    for condition, copy in pending:
        if condition is None:
            copy.wait_send()
        else:
            pl.when(condition)(copy.wait_send)


def exchange(vectors, values, counts, snps, scores):
    devices = lax.axis_size("panel")
    piece, depth = vectors.shape
    blocks, snp_rows, width = scores.shape[1:]
    row_total = devices * piece
    pair_rows = 4 * piece
    place = lax.rem(lax.axis_index("panel"), 4) * piece
    rider = jnp.zeros((8, pair_rows), jnp.float32)
    spread = jnp.broadcast_to(values.astype(jnp.float32), (8, piece))
    rider = lax.dynamic_update_slice_in_dim(rider, spread, place, 1)
    halves = 2
    chunks = blocks // 2
    vmem = pl.BlockSpec(memory_space=pltpu.VMEM)
    smem = pl.BlockSpec(memory_space=pltpu.SMEM)
    return pl.pallas_call(
        exchange_kernel,
        out_shape=jax.ShapeDtypeStruct((ROUNDS + 1, 1, blocks, width, width), jnp.float32),
        in_specs=[smem, smem, vmem, vmem, vmem],
        out_specs=vmem,
        scratch_shapes=[
            pltpu.VMEM((devices, row_total, width), jnp.bfloat16),
            pltpu.VMEM((devices, 8, pair_rows), jnp.float32),
            pltpu.VMEM((chunks, 2 * width, pair_rows), jnp.bfloat16),
            pltpu.VMEM((row_total, depth), jnp.bfloat16),
            pltpu.VMEM((blocks // 2, snp_rows, 2 * width), jnp.bfloat16),
            pltpu.SemaphoreType.DMA((2,)),
            pltpu.SemaphoreType.DMA((4, devices, halves)),
            pltpu.SemaphoreType.DMA((devices, halves)),
            pltpu.SemaphoreType.DMA((4, devices, chunks)),
            pltpu.SemaphoreType.DMA((devices, chunks)),
            pltpu.SemaphoreType.DMA((devices,)),
            pltpu.SemaphoreType.DMA((devices,)),
        ],
        compiler_params=pltpu.CompilerParams(
            collective_id=0, has_side_effects=True, vmem_limit_bytes=LIMIT
        ),
    )(counts, snps, vectors, rider, scores)


def per_device(eig_vectors, eig_values, eig_count, snp_count, zscores, samples):
    devices = lax.axis_size("panel")
    spacing = max(1, devices // 32)
    panels = devices // spacing
    slot_index = lax.axis_index("panel")
    panel_index = slot_index // spacing
    group_index = slot_index % spacing
    blocks_here, snp_rows, panel_width = zscores.shape[1:]
    counts = lax.dynamic_slice_in_dim(eig_count, group_index * blocks_here, blocks_here)
    snps = lax.dynamic_slice_in_dim(snp_count, group_index * blocks_here, blocks_here)
    rounds = jnp.arange(ROUNDS + 1, dtype=jnp.int32)
    partners = (panel_index - rounds) % panels
    scales = samples.astype(jnp.float32).reshape(panels, panel_width)
    own_scale = lax.dynamic_index_in_dim(scales, panel_index, 0, keepdims=False)
    scale = 1.0 / jnp.sqrt(own_scale[None, :, None] * scales[partners][:, None, :])

    if spacing == 1 and panels == 2 * ROUNDS and blocks_here == panels // 2:
        raw = exchange(eig_vectors, eig_values, counts, snps, zscores)
        return raw * scale[:, None, None]
    members = [[g + spacing * i for i in range(panels)] for g in range(spacing)]
    gather = functools.partial(
        lax.all_gather, axis_name="panel", axis_index_groups=members if spacing > 1 else None
    )
    vectors = gather(eig_vectors, tiled=True)
    values = gather(eig_values, tiled=True)
    projected = project(vectors, zscores, counts, snps)
    held = gather(projected)
    weighted = (projected.astype(jnp.float32) / values.astype(jnp.float32)[:, None]).astype(
        jnp.bfloat16
    )
    return grams(weighted, held, scale, partners, counts)


def solution(mesh):
    placed = (
        P(("groups", "panel"), None),
        P(("groups", "panel")),
        P("groups"),
        P("groups"),
        P(("groups", "panel"), None, None, None),
        P("groups"),
    )
    return jax.shard_map(
        per_device,
        mesh=mesh,
        in_specs=placed,
        out_specs=P(None, ("groups", "panel"), None, None, None),
        check_vma=False,
    )
```

profile of v0, /device:TPU:0, one launch (start us, length us, event | category | flops | bytes accessed | tf_op | source)
XLA Modules:
  0.0 104.1 jit_solution(7179943406357883581)
XLA Ops:
  0.0 0.0 copy-start.1
  0.0 0.7 broadcast_in_dim.5
  0.7 0.2 dynamic_update_slice.3.own_values
  0.9 0.0 copy-start
  0.9 0.6 copy-done
  1.5 96.4 %shard_map.64 = f32[9,1,8,128,128]{4,3,2,1,0:T(8,128)} custom-call(s32[8]{0:T(128)} %counts, s32[8]{0:T(128)} %snps, bf16[160,1024]{1,0:T(8,128)(2,1)} %own.1, f32[8,640]{1,0:T(8,128)} %copy-done, bf16[1,8,1024,128]{3,2,1,0:T(8,128)(2,1)} %scores.1), custom_call_target="tpu_custom_call" | custom-call | tf_op jit(solution)/shard_map/pallas_call | solution.py:350
  97.9 0.0 copy-done.1
  98.0 0.6 gather_fusion
  98.5 0.2 multiply_rsqrt_fusion
  98.7 5.4 %broadcast_multiply_fusion = f32[9,1,8,128,128]{4,3,2,1,0:T(8,128)} fusion(f32[9,1,8,128,128]{4,3,2,1,0:T(8,128)} %shard_map.64, f32[9,128,128]{2,1,0:T(8,128)S(1)} %multiply_rsqrt_fusion), kind=kLoop, calls=%fused_computation.1 | loop fusion | flops 1179648 | bytes 10027008 | tf_op jit(solution)/shard_map/mul | solution.py:393
  (5 shorter events, 0.0 us)
Async XLA Ops:
  0.0 97.9 %copy-start.1 = (bf16[2048]{0:T(1024)(128)(2,1)S(1)}, bf16[2048]{0:T(1024)(128)(2,1)}, u32[]{:S(2)}) copy-start(bf16[2048]{0:T(1024)(128)(2,1)} %param.11) | copy-start | bytes 12292
  0.9 0.6 copy-start
where the time goes:
time: 104 us
  Pallas kernels  96.4 us (93%)
  other arithmetic  5.61 us (5%)
  local copies, waits for them, and re-layouts  2.06 us (2%)
    pallas_call x1, Pallas kernels, exchange(): pl.pallas_call(exchange_kernel, out_shape=jax.ShapeDtypeStruct((ROUNDS +...  96.4 us
    mul x1, other arithmetic, per_device(): return raw * scale[:, None, None]  5.43 us

commit v1 on v0

v1 whole, which is shorter than its diff:
```python
import functools

import jax
import jax.numpy as jnp
from jax import lax
from jax.experimental import pallas as pl
from jax.experimental.pallas import tpu as pltpu
from jax.sharding import PartitionSpec as P

ROUNDS = 8
LIMIT = 56 * 1024 * 1024
EXCHANGE_LIMIT = 36 * 1024 * 1024


def place_masked(snps, scores, pair, store):
    width = scores.shape[-1]
    for side in range(2):
        block = 2 * pair + side
        rows = lax.broadcasted_iota(jnp.int32, scores.shape[-2:], 0)
        part = jnp.where(rows < snps[block], scores[side].astype(jnp.float32), 0.0)
        store[:, side * width : (side + 1) * width] = part.astype(jnp.bfloat16)


def project_rows(vectors, masked, first_count):
    both = jnp.dot(vectors, masked, preferred_element_type=jnp.float32)
    width = both.shape[1] // 2
    rows = lax.broadcasted_iota(jnp.int32, (both.shape[0], width), 0)
    return jnp.where(rows < first_count, both[:, :width], both[:, width:]).astype(jnp.bfloat16)


def project_kernel(counts, snps, vectors, scores, out, masked):
    pair = pl.program_id(0)
    place_masked(snps, scores.at[0], pair, masked)
    out[...] = project_rows(vectors[...], masked[...], counts[2 * pair])


def project(vectors, scores, counts, snps):
    row_total, depth = vectors.shape
    blocks, snp_rows, width = scores.shape[1:]
    pair_rows = 2 * row_total // blocks
    return pl.pallas_call(
        project_kernel,
        out_shape=jax.ShapeDtypeStruct((row_total, width), jnp.bfloat16),
        grid_spec=pltpu.PrefetchScalarGridSpec(
            num_scalar_prefetch=2,
            grid=(blocks // 2,),
            in_specs=[
                pl.BlockSpec((pair_rows, depth), lambda b, *_: (b, 0)),
                pl.BlockSpec((1, 2, snp_rows, width), lambda b, *_: (0, b, 0, 0)),
            ],
            out_specs=pl.BlockSpec((pair_rows, width), lambda b, *_: (b, 0)),
            scratch_shapes=[pltpu.VMEM((snp_rows, 2 * width), jnp.bfloat16)],
        ),
        compiler_params=pltpu.CompilerParams(vmem_limit_bytes=LIMIT),
    )(counts, snps, vectors, scores)


def gram_kernel(counts, slots, weighted, panels, scale, out):
    pair = pl.program_id(0)
    width = weighted.shape[1]
    left = weighted[...].astype(jnp.float32)
    rows = lax.broadcasted_iota(jnp.int32, left.shape, 0)
    first = rows < counts[2 * pair]
    left = jnp.concatenate([jnp.where(first, left, 0.0).T, jnp.where(first, 0.0, left).T], axis=0)
    left = left.astype(jnp.bfloat16)
    shape = (width, width)
    same = lax.broadcasted_iota(jnp.int32, shape, 0) == lax.broadcasted_iota(jnp.int32, shape, 1)
    for index in range(out.shape[0]):
        both = jnp.dot(left, panels[slots[index]], preferred_element_type=jnp.float32)
        for side in range(2):
            gram = both[side * width : (side + 1) * width]
            if index == 0:
                count = counts[2 * pair + side].astype(jnp.float32)
                gram = gram - jnp.where(same, count, 0.0)
            out[index, 0, side] = gram * scale[index]


def grams(weighted, panels, scale, slots, counts):
    blocks = counts.shape[0]
    rounds, width = scale.shape[:2]
    pair_rows = 2 * weighted.shape[0] // blocks
    return pl.pallas_call(
        gram_kernel,
        out_shape=jax.ShapeDtypeStruct((rounds, 1, blocks, width, width), jnp.float32),
        grid_spec=pltpu.PrefetchScalarGridSpec(
            num_scalar_prefetch=2,
            grid=(blocks // 2,),
            in_specs=[
                pl.BlockSpec((pair_rows, width), lambda b, *_: (b, 0)),
                pl.BlockSpec((panels.shape[0], pair_rows, width), lambda b, *_: (0, b, 0)),
                pl.BlockSpec(scale.shape, lambda b, *_: (0, 0, 0)),
            ],
            out_specs=pl.BlockSpec((rounds, 1, 2, width, width), lambda b, *_: (0, 0, b, 0, 0)),
        ),
        compiler_params=pltpu.CompilerParams(vmem_limit_bytes=LIMIT),
    )(counts, slots, weighted, panels, scale)


def exchange_kernel(counts, snps, own, own_values, scores, out, held, values, left, store, raw,
                    masked, here, load, send1, recv1, send2, recv2):
    line = lax.axis_size("panel") // 4
    me = lax.axis_index("panel")
    z = me // 4
    y = (me // 2) % 2
    k = me % 2
    piece = own.shape[0]
    pair_rows = 4 * piece
    parts = recv1.shape[1]
    part_rows = piece // (parts - 1)
    chunks = recv2.shape[1]
    top = line - 1
    inner = (z > 0) & (z < top)
    edge = (z == 0) | (z == top)
    up, down, across, beside = me + 4, me - 4, me + 2 - 4 * y, me + 1 - 2 * k
    skip = me + 8 - 16 * (z // 2)
    pending = []

    def order(plane, step):
        near = jnp.minimum(plane, top - plane)
        nearest = jnp.where(step > 2 * near, step, (near + (step + 1) // 2 * (1 - 2 * (step % 2))))
        return jnp.where(plane > top - plane, top - nearest, nearest)

    loads = []
    for step in range(line):
        pair = pl.ds(2 * order(z, step), 2)
        loads.append(
            pltpu.make_async_copy(scores.at[0, pair], raw.at[pl.ds(2 * step, 2)], load.at[step])
        )
    local = [
        pltpu.make_async_copy(own, store.at[pl.ds(me * piece, piece)], here.at[0]),
        pltpu.make_async_copy(own_values, values.at[me], here.at[1]),
    ]
    for copy in local + loads:
        copy.start()

    barrier = pltpu.get_barrier_semaphore()

    def greet(target):
        pl.semaphore_signal(
            barrier, inc=1, device_id={"panel": target}, device_id_type=pl.DeviceIdType.MESH
        )

    pl.when(z < top)(functools.partial(greet, up))
    pl.when(z > 0)(functools.partial(greet, down))
    for target in (across, beside, skip):
        greet(target)
    pl.semaphore_wait(barrier, jnp.where(inner, 5, 4))

    def start(condition, copy):
        if condition is None:
            copy.start()
        else:
            pl.when(condition)(copy.start)
        pending.append((condition, copy))

    def remote(source, target, send, recv, device):
        return pltpu.make_async_remote_copy(
            src_ref=source,
            dst_ref=target,
            send_sem=send,
            recv_sem=recv,
            device_id={"panel": device},
            device_id_type=pl.DeviceIdType.MESH,
        )

    def move1(source, part, way, target, first=False):
        sems = send1.at[way, source, part], recv1.at[source, part]
        if part == parts - 1:
            origin = own_values if first else values.at[source]
            return remote(origin, values.at[source], *sems, target)
        rows = pl.ds(source * piece + part * part_rows, part_rows)
        origin = own.at[pl.ds(part * part_rows, part_rows)] if first else store.at[rows]
        return remote(origin, store.at[rows], *sems, target)

    def arrive1(source, part):
        move1(source, part, 0, beside).wait_recv()

    def move2(source, chunk, way, target):
        block = held.at[source, pl.ds(chunk * pair_rows, pair_rows)]
        return remote(block, block, send2.at[way, source, chunk], recv2.at[source, chunk], target)

    def arrive2(source, chunk):
        move2(source, chunk, 0, beside).wait_recv()

    def both(a, b):
        return b if a is None else a & b

    def column(step, condition=None):
        plane = order(z, step)
        source = plane * 4 + y * 2 + k
        for part in range(parts):
            if condition is None:
                arrive1(source, part)
            else:
                pl.when(condition)(functools.partial(arrive1, source, part))
            start(both(condition, (plane < z) & (z < top)), move1(source, part, 0, up))
            start(both(condition, (plane > z) & (z > 0)), move1(source, part, 1, down))
            start(condition, move1(source, part, 2, across))
            start(condition, move1(source, part, 3, beside))

    def sideways(step):
        source = order(z, step) * 4 + 2 - 2 * y + k
        for part in range(parts):
            arrive1(source, part)
            start(None, move1(source, part, 3, beside))

    def mask(step):
        loads[step].wait()
        place_masked(snps, raw.at[pl.ds(2 * step, 2)], order(z, step), masked.at[step])

    def finish(step):
        plane = order(z, step)
        for source in (plane * 4 + y * 2 + 1 - k, plane * 4 + 2 - 2 * y + 1 - k):
            for part in range(parts):
                arrive1(source, part)
        rows = pl.ds(plane * pair_rows, pair_rows)
        held[me, rows] = project_rows(store[rows], masked[step], counts[2 * plane])
        start(z < top, move2(me, plane, 0, up))
        start(z >= 2, move2(me, plane, 1, skip))
        start(k == 0, move2(me, plane, 3, beside))
        weigh(plane)

    def weigh(index):
        rows = pl.ds(index * pair_rows, pair_rows)
        row = values[4 * index] + values[4 * index + 1]
        row = row + (values[4 * index + 2] + values[4 * index + 3])
        flat = held[me, rows].astype(jnp.float32).T / row
        first = lax.broadcasted_iota(jnp.int32, flat.shape, 1) < counts[2 * index]
        both = jnp.concatenate([jnp.where(first, flat, 0.0), jnp.where(first, 0.0, flat)], axis=0)
        left[index] = both.astype(jnp.bfloat16)

    def plane_behind(lag):
        return lax.rem(z - lag + line, line)

    def own_across(step):
        start(y == 0, move2(me, order(z, step), 2, across))

    def relay(step):
        for turn in range(2):
            lag = jnp.where(z == 0, 2 - turn, 1 + turn)
            plane = plane_behind(lag)
            source = plane * 4 + y * 2 + k
            chunk = order(plane, step)
            arrive2(source, chunk)
            start((lag == 1) & inner, move2(source, chunk, 0, up))
            start((lag == 2) & (z == 1), move2(source, chunk, 1, down))
            start((lag == 1) | (y == 1), move2(source, chunk, 2, across))
            start((lag == 1) | (k == 1), move2(source, chunk, 3, beside))

    cross = [plane_behind(lag + 1 - y) * 4 + (1 - y) * 2 + k for lag in range(2)]
    near = [plane_behind(lag) * 4 + y * 2 + k for lag in range(3)]
    swap = 1 - 2 * k

    def cross_over(step):
        for source in cross:
            chunk = order(source // 4, step)
            arrive2(source, chunk)
            start(None, move2(source, chunk, 3, beside))

    def gram(source, step, number, own_panel=False):
        chunk = order(source // 4, step)
        rows = pl.ds(chunk * pair_rows, pair_rows)
        both = jnp.dot(left[chunk], held[source, rows], preferred_element_type=jnp.float32)
        width = both.shape[1]
        for side in range(2):
            part = both[side * width : (side + 1) * width]
            if own_panel:
                shape = (width, width)
                across_rows = lax.broadcasted_iota(jnp.int32, shape, 0)
                same = across_rows == lax.broadcasted_iota(jnp.int32, shape, 1)
                count = counts[2 * chunk + side].astype(jnp.float32)
                part = part - jnp.where(same, count, 0.0)
            out[number, 0, 2 * chunk + side] = part

    def grams_near(step):
        for lag, source in enumerate(near):
            gram(source, step, 4 * lag, lag == 0)

    def grams_near_beside(step):
        for lag, source in enumerate(near):
            number = 4 * lag - swap

            @pl.when((number >= 0) & (number < out.shape[0]))
            def _():
                arrive2(source + swap, order(source // 4, step))
                gram(source + swap, step, number)

    def grams_cross(step):
        for lag, source in enumerate(cross):
            gram(source, step, 4 * lag + 2)

    def grams_cross_beside(step):
        for lag, source in enumerate(cross):
            arrive2(source + swap, order(source // 4, step))
            gram(source + swap, step, 4 * lag + 2 - swap)

    for part in range(parts):
        start(z < top, move1(me, part, 0, up, True))
        start(z > 0, move1(me, part, 1, down, True))
        start(None, move1(me, part, 2, across, True))
        start(None, move1(me, part, 3, beside, True))
    mask(0)
    for copy in local:
        copy.wait()
    column(1)
    column(2, inner)
    sideways(0)
    finish(0)
    mask(1)
    column(2, edge)
    column(3, inner)
    sideways(1)
    finish(1)
    mask(2)
    column(3, edge)
    mask(3)
    sideways(2)
    own_across(0)
    finish(2)
    relay(0)
    sideways(3)
    finish(3)
    own_across(1)
    relay(1)
    cross_over(0)
    grams_near(0)
    grams_near_beside(0)
    own_across(2)
    relay(2)
    cross_over(1)
    grams_cross(0)
    grams_cross_beside(0)
    grams_near(1)
    grams_near_beside(1)
    own_across(3)
    relay(3)
    cross_over(2)
    grams_cross(1)
    grams_cross_beside(1)
    grams_near(2)
    grams_near_beside(2)
    grams_near(3)
    grams_near_beside(3)
    grams_cross(2)
    cross_over(3)
    grams_cross_beside(2)
    grams_cross(3)
    grams_cross_beside(3)
    for condition, copy in pending:
        if condition is None:
            copy.wait_send()
        else:
            pl.when(condition)(copy.wait_send)


def exchange(vectors, values, counts, snps, scores):
    devices = lax.axis_size("panel")
    piece, depth = vectors.shape
    blocks, snp_rows, width = scores.shape[1:]
    row_total = devices * piece
    pair_rows = 4 * piece
    place = lax.rem(lax.axis_index("panel"), 4)
    lanes = jnp.arange(pair_rows, dtype=jnp.int32) // piece
    rider = jnp.where(lanes == place, jnp.tile(values.astype(jnp.float32), 4), 0.0)[None]
    parts = 3
    chunks = blocks // 2
    vmem = pl.BlockSpec(memory_space=pltpu.VMEM)
    smem = pl.BlockSpec(memory_space=pltpu.SMEM)
    anywhere = pl.BlockSpec(memory_space=pltpu.HBM)
    return pl.pallas_call(
        exchange_kernel,
        out_shape=jax.ShapeDtypeStruct((ROUNDS + 1, 1, blocks, width, width), jnp.float32),
        in_specs=[smem, smem, anywhere, anywhere, anywhere],
        out_specs=vmem,
        scratch_shapes=[
            pltpu.VMEM((devices, row_total, width), jnp.bfloat16),
            pltpu.VMEM((devices, 1, pair_rows), jnp.float32),
            pltpu.VMEM((chunks, 2 * width, pair_rows), jnp.bfloat16),
            pltpu.VMEM((row_total, depth), jnp.bfloat16),
            pltpu.VMEM((blocks, snp_rows, width), jnp.bfloat16),
            pltpu.VMEM((chunks, snp_rows, 2 * width), jnp.bfloat16),
            pltpu.SemaphoreType.DMA((2,)),
            pltpu.SemaphoreType.DMA((chunks,)),
            pltpu.SemaphoreType.DMA((4, devices, parts)),
            pltpu.SemaphoreType.DMA((devices, parts)),
            pltpu.SemaphoreType.DMA((4, devices, chunks)),
            pltpu.SemaphoreType.DMA((devices, chunks)),
        ],
        compiler_params=pltpu.CompilerParams(
            collective_id=0, has_side_effects=True, vmem_limit_bytes=EXCHANGE_LIMIT
        ),
    )(counts, snps, vectors, rider, scores)


def per_device(eig_vectors, eig_values, eig_count, snp_count, zscores, samples):
    devices = lax.axis_size("panel")
    spacing = max(1, devices // 32)
    panels = devices // spacing
    slot_index = lax.axis_index("panel")
    panel_index = slot_index // spacing
    group_index = slot_index % spacing
    blocks_here, snp_rows, panel_width = zscores.shape[1:]
    counts = lax.dynamic_slice_in_dim(eig_count, group_index * blocks_here, blocks_here)
    snps = lax.dynamic_slice_in_dim(snp_count, group_index * blocks_here, blocks_here)
    rounds = jnp.arange(ROUNDS + 1, dtype=jnp.int32)
    partners = (panel_index - rounds) % panels
    scales = samples.astype(jnp.float32).reshape(panels, panel_width)
    own_scale = lax.dynamic_index_in_dim(scales, panel_index, 0, keepdims=False)
    scale = 1.0 / jnp.sqrt(own_scale[None, :, None] * scales[partners][:, None, :])

    if spacing == 1 and panels == 2 * ROUNDS and blocks_here == panels // 2:
        raw = exchange(eig_vectors, eig_values, counts, snps, zscores)
        return raw * scale[:, None, None]
    members = [[g + spacing * i for i in range(panels)] for g in range(spacing)]
    gather = functools.partial(
        lax.all_gather, axis_name="panel", axis_index_groups=members if spacing > 1 else None
    )
    vectors = gather(eig_vectors, tiled=True)
    values = gather(eig_values, tiled=True)
    projected = project(vectors, zscores, counts, snps)
    held = gather(projected)
    weighted = (projected.astype(jnp.float32) / values.astype(jnp.float32)[:, None]).astype(
        jnp.bfloat16
    )
    return grams(weighted, held, scale, partners, counts)


def solution(mesh):
    placed = (
        P(("groups", "panel"), None),
        P(("groups", "panel")),
        P("groups"),
        P("groups"),
        P(("groups", "panel"), None, None, None),
        P("groups"),
    )
    return jax.shard_map(
        per_device,
        mesh=mesh,
        in_specs=placed,
        out_specs=P(None, ("groups", "panel"), None, None, None),
        check_vma=False,
    )
```

time: 104 us -> 87.1 us (0.84)
  Pallas kernels: 96.4 us -> 78.1 us
  local copies, waits for them, and re-layouts: 2.06 us -> 5.18 us
  other arithmetic: 5.61 us -> 3.52 us
    pallas_call x1, Pallas kernels: 96.4 us -> 78.1 us  [exchange(): pl.pallas_call(exchange_kernel, out_shape=jax.ShapeDtypeStruct((ROUNDS +...]
    unnamed x4 -> x8, local copies, waits for them, and re-layouts: 0.6 us -> 3.87 us
    mul x1, other arithmetic: 5.43 us -> 2.63 us  [per_device(): return raw * scale[:, None, None]]
where the time goes in v1:
time: 87.1 us; the launch traced here: 86.9 us
  Pallas kernels  78.1 us (90%)
  local copies, waits for them, and re-layouts  5.18 us (6%)
  other arithmetic  3.52 us (4%)
    pallas_call x1, Pallas kernels, exchange(): pl.pallas_call(exchange_kernel, out_shape=jax.ShapeDtypeStruct((ROUNDS +...  78.1 us
    unnamed x8, local copies, waits for them, and re-layouts  3.87 us
    mul x1, other arithmetic, per_device(): return raw * scale[:, None, None]  2.63 us

profile of v1, /device:TPU:0, one launch (start us, length us, event | category | flops | bytes accessed | tf_op | source)
XLA Modules:
  0.0 86.9 jit_solution(4461304915568947356)
XLA Ops:
  0.0 0.7 tile.4
  0.7 0.1 tile.10
  0.8 0.7 bitcast_convert_fusion
  1.5 0.6 gather_fusion
  2.1 0.2 multiply_rsqrt_fusion
  2.2 0.0 copy-start
  2.2 1.6 %copy-done = bf16[1,8,1024,128]{3,2,1,0:T(8,128)(2,1)S(1)} copy-done((bf16[1,8,1024,128]{3,2,1,0:T(8,128)(2,1)S(1)}, bf16[1,8,1024,128]{3,2,1,0:T(8,128)(2,1)}, u32[]{:S(2)}) %copy-start) | copy-done | bytes 2097176
  3.8 0.0 copy-start.1
  3.8 1.0 %copy-done.1 = bf16[160,1024]{1,0:T(8,128)(2,1)S(1)} copy-done((bf16[160,1024]{1,0:T(8,128)(2,1)S(1)}, bf16[160,1024]{1,0:T(8,128)(2,1)}, u32[]{:S(2)}) %copy-start.1) | copy-done | bytes 327704
  4.8 0.0 copy-start.2
  4.8 0.7 copy-done.2
  5.4 0.0 copy-start.3
  5.4 0.7 copy-done.3
  6.1 78.1 %shard_map.64 = f32[9,1,8,128,128]{4,3,2,1,0:T(8,128)S(1)} custom-call(s32[8]{0:T(128)S(1)} %copy-done.2, s32[8]{0:T(128)S(1)} %copy-done.3, bf16[160,1024]{1,0:T(8,128)(2,1)S(1)} %copy-done.1, f32[1,640]{1,0:T(1,128)S(1)} %compare_select_fusion.own_values, bf16[1,8,1024,128]{3,2,1,0:T(8,128)(2,1)S(1)} %copy-done), custom_call_target="tpu_custom_call" | custom-call | tf_op jit(solution)/shard_map/pallas_call | solution.py:370
  84.2 2.6 %broadcast_multiply_fusion = f32[9,1,8,128,128]{4,3,2,1,0:T(8,128)} fusion(f32[9,1,8,128,128]{4,3,2,1,0:T(8,128)S(1)} %shard_map.64, f32[9,128,128]{2,1,0:T(8,128)S(1)} %multiply_rsqrt_fusion), kind=kLoop, calls=%fused_computation.1 | loop fusion | flops 1179648 | bytes 10027008 | tf_op jit(solution)/shard_map/mul | solution.py:413
  (4 shorter events, 0.0 us)
Async XLA Ops:
  2.2 1.6 %copy-start = (bf16[1,8,1024,128]{3,2,1,0:T(8,128)(2,1)S(1)}, bf16[1,8,1024,128]{3,2,1,0:T(8,128)(2,1)}, u32[]{:S(2)}) copy-start(bf16[1,8,1024,128]{3,2,1,0:T(8,128)(2,1)} %scores.1) | copy-start | bytes 6291460
  3.8 1.0 %copy-start.1 = (bf16[160,1024]{1,0:T(8,128)(2,1)S(1)}, bf16[160,1024]{1,0:T(8,128)(2,1)}, u32[]{:S(2)}) copy-start(bf16[160,1024]{1,0:T(8,128)(2,1)} %own.1) | copy-start | bytes 983044
  4.8 0.7 copy-start.2
  5.4 0.7 copy-start.3

commit v2 on v1

--- a/solution.py
+++ b/solution.py
@@ -96,8 +96,9 @@
     )(counts, slots, weighted, panels, scale)
 
 
-def exchange_kernel(counts, snps, own, own_values, scores, out, held, values, left, store, raw,
-                    masked, here, load, send1, recv1, send2, recv2):
+def exchange_kernel(all_counts, all_snps, own, own_values, samples, scores, out, scale, counts, snps,
+                    flat_values, units, held, values, left, store, raw, masked, here, load,
+                    send1, recv1, send2, recv2):
     line = lax.axis_size("panel") // 4
     me = lax.axis_index("panel")
     z = me // 4
@@ -128,7 +129,10 @@
         )
     local = [
         pltpu.make_async_copy(own, store.at[pl.ds(me * piece, piece)], here.at[0]),
-        pltpu.make_async_copy(own_values, values.at[me], here.at[1]),
+        pltpu.make_async_copy(own_values, flat_values, here.at[1]),
+        pltpu.make_async_copy(all_counts, counts, here.at[2]),
+        pltpu.make_async_copy(all_snps, snps, here.at[3]),
+        pltpu.make_async_copy(samples, units, here.at[4]),
     ]
     for copy in local + loads:
         copy.start()
@@ -142,9 +146,19 @@
 
     pl.when(z < top)(functools.partial(greet, up))
     pl.when(z > 0)(functools.partial(greet, down))
-    for target in (across, beside, skip):
+    pl.when(z < 2)(functools.partial(greet, skip))
+    for target in (across, beside):
         greet(target)
-    pl.semaphore_wait(barrier, jnp.where(inner, 5, 4))
+    for copy in local[1:]:
+        copy.wait()
+    spot = lax.broadcasted_iota(jnp.int32, (piece, pair_rows), 1) - lax.rem(me, 4) * piece
+    hot = jnp.where(spot == lax.broadcasted_iota(jnp.int32, spot.shape, 0), 1.0, 0.0)
+    ride = jnp.broadcast_to(flat_values[...].astype(jnp.float32).reshape(1, piece), (8, piece))
+    ride = jnp.dot(
+        ride.astype(jnp.bfloat16), hot.astype(jnp.bfloat16), preferred_element_type=jnp.float32
+    )
+    values[me] = ride[0:1]
+    pl.semaphore_wait(barrier, 2 + jnp.where(z > 0, 1, 0) + jnp.where(z < top, 1, 0) + z // 2)
 
     def start(condition, copy):
         if condition is None:
@@ -166,8 +180,7 @@
     def move1(source, part, way, target, first=False):
         sems = send1.at[way, source, part], recv1.at[source, part]
         if part == parts - 1:
-            origin = own_values if first else values.at[source]
-            return remote(origin, values.at[source], *sems, target)
+            return remote(values.at[source], values.at[source], *sems, target)
         rows = pl.ds(source * piece + part * part_rows, part_rows)
         origin = own.at[pl.ds(part * part_rows, part_rows)] if first else store.at[rows]
         return remote(origin, store.at[rows], *sems, target)
@@ -216,7 +229,6 @@
         rows = pl.ds(plane * pair_rows, pair_rows)
         held[me, rows] = project_rows(store[rows], masked[step], counts[2 * plane])
         start(z < top, move2(me, plane, 0, up))
-        start(z >= 2, move2(me, plane, 1, skip))
         start(k == 0, move2(me, plane, 3, beside))
         weigh(plane)
 
@@ -229,23 +241,41 @@
         both = jnp.concatenate([jnp.where(first, flat, 0.0), jnp.where(first, 0.0, flat)], axis=0)
         left[index] = both.astype(jnp.bfloat16)
 
+    def scales():
+        table = units[...].astype(jnp.float32)
+        panels = lax.broadcasted_iota(jnp.int32, table.shape, 0)
+
+        def row(panel):
+            return jnp.sum(jnp.where(panels == panel, table, 0.0), axis=0, keepdims=True)
+
+        width = table.shape[1]
+        mine = jnp.broadcast_to(row(me), (width, width)).T
+        for number in range(out.shape[0]):
+            partner = lax.rem(me - number + 4 * line, 4 * line)
+            scale[number] = 1.0 / jnp.sqrt(mine * row(partner))
+
     def plane_behind(lag):
         return lax.rem(z - lag + line, line)
 
     def own_across(step):
         start(y == 0, move2(me, order(z, step), 2, across))
 
-    def relay(step):
-        for turn in range(2):
-            lag = jnp.where(z == 0, 2 - turn, 1 + turn)
-            plane = plane_behind(lag)
-            source = plane * 4 + y * 2 + k
-            chunk = order(plane, step)
+    def far(step):
+        start(z >= 2, move2(me, order(z, step), 1, skip))
+
+    def relay(step, turn, condition=None):
+        lag = jnp.where(z == 0, 2 - turn, 1 + turn)
+        plane = plane_behind(lag)
+        source = plane * 4 + y * 2 + k
+        chunk = order(plane, step)
+        if condition is None:
             arrive2(source, chunk)
-            start((lag == 1) & inner, move2(source, chunk, 0, up))
-            start((lag == 2) & (z == 1), move2(source, chunk, 1, down))
-            start((lag == 1) | (y == 1), move2(source, chunk, 2, across))
-            start((lag == 1) | (k == 1), move2(source, chunk, 3, beside))
+        else:
+            pl.when(condition)(functools.partial(arrive2, source, chunk))
+        start(both(condition, (lag == 1) & inner), move2(source, chunk, 0, up))
+        start(both(condition, (lag == 2) & (z == 1)), move2(source, chunk, 1, down))
+        start(both(condition, (lag == 1) | (y == 1)), move2(source, chunk, 2, across))
+        start(both(condition, (lag == 1) | (k == 1)), move2(source, chunk, 3, beside))
 
     cross = [plane_behind(lag + 1 - y) * 4 + (1 - y) * 2 + k for lag in range(2)]
     near = [plane_behind(lag) * 4 + y * 2 + k for lag in range(3)]
@@ -300,50 +330,60 @@
         start(None, move1(me, part, 2, across, True))
         start(None, move1(me, part, 3, beside, True))
     mask(0)
-    for copy in local:
-        copy.wait()
+    local[0].wait()
+    mask(1)
+    mask(2)
+    mask(3)
+    scales()
     column(1)
     column(2, inner)
     sideways(0)
     finish(0)
-    mask(1)
     column(2, edge)
     column(3, inner)
     sideways(1)
     finish(1)
-    mask(2)
+    far(0)
+    far(1)
+    relay(0, 0, inner)
     column(3, edge)
-    mask(3)
+    own_across(0)
     sideways(2)
-    own_across(0)
     finish(2)
-    relay(0)
+    far(2)
+    relay(0, 1, inner)
+    relay(0, 0, edge)
     sideways(3)
     finish(3)
+    far(3)
     own_across(1)
-    relay(1)
+    relay(0, 1, edge)
+    relay(1, 0)
+    grams_near(0)
+    relay(1, 1)
     cross_over(0)
-    grams_near(0)
+    own_across(2)
     grams_near_beside(0)
-    own_across(2)
-    relay(2)
+    relay(2, 0)
+    grams_cross(0)
+    relay(2, 1)
     cross_over(1)
-    grams_cross(0)
+    own_across(3)
+    grams_near(1)
     grams_cross_beside(0)
-    grams_near(1)
+    relay(3, 0)
     grams_near_beside(1)
-    own_across(3)
-    relay(3)
+    grams_cross(1)
+    relay(3, 1)
     cross_over(2)
-    grams_cross(1)
     grams_cross_beside(1)
     grams_near(2)
     grams_near_beside(2)
+    grams_cross(2)
     grams_near(3)
     grams_near_beside(3)
-    grams_cross(2)
+    grams_cross_beside(2)
     cross_over(3)
-    grams_cross_beside(2)
     grams_cross(3)
     grams_cross_beside(3)
     for condition, copy in pending:
@@ -353,33 +393,37 @@
             pl.when(condition)(copy.wait_send)
 
 
-def exchange(vectors, values, counts, snps, scores):
+def exchange(vectors, values, samples, counts, snps, scores):
     devices = lax.axis_size("panel")
     piece, depth = vectors.shape
     blocks, snp_rows, width = scores.shape[1:]
     row_total = devices * piece
     pair_rows = 4 * piece
-    place = lax.rem(lax.axis_index("panel"), 4)
-    lanes = jnp.arange(pair_rows, dtype=jnp.int32) // piece
-    rider = jnp.where(lanes == place, jnp.tile(values.astype(jnp.float32), 4), 0.0)[None]
     parts = 3
     chunks = blocks // 2
-    vmem = pl.BlockSpec(memory_space=pltpu.VMEM)
-    smem = pl.BlockSpec(memory_space=pltpu.SMEM)
-    anywhere = pl.BlockSpec(memory_space=pltpu.HBM)
+    rounds = ROUNDS + 1
+    hbm = pl.BlockSpec(memory_space=pltpu.HBM)
+    operands = [counts, snps, vectors, values, samples.reshape(devices, width), scores]
     return pl.pallas_call(
         exchange_kernel,
-        out_shape=jax.ShapeDtypeStruct((ROUNDS + 1, 1, blocks, width, width), jnp.float32),
-        in_specs=[smem, smem, anywhere, anywhere, anywhere],
-        out_specs=vmem,
+        out_shape=[
+            jax.ShapeDtypeStruct((rounds, 1, blocks, width, width), jnp.float32),
+            jax.ShapeDtypeStruct((rounds, width, width), jnp.float32),
+        ],
+        in_specs=[hbm] * len(operands),
+        out_specs=[pl.BlockSpec(memory_space=pltpu.VMEM)] * 2,
         scratch_shapes=[
+            pltpu.SMEM((blocks,), jnp.int32),
+            pltpu.SMEM((blocks,), jnp.int32),
+            pltpu.VMEM((piece,), jnp.bfloat16),
+            pltpu.VMEM((devices, width), jnp.bfloat16),
             pltpu.VMEM((devices, row_total, width), jnp.bfloat16),
             pltpu.VMEM((devices, 1, pair_rows), jnp.float32),
             pltpu.VMEM((chunks, 2 * width, pair_rows), jnp.bfloat16),
             pltpu.VMEM((row_total, depth), jnp.bfloat16),
             pltpu.VMEM((blocks, snp_rows, width), jnp.bfloat16),
             pltpu.VMEM((chunks, snp_rows, 2 * width), jnp.bfloat16),
-            pltpu.SemaphoreType.DMA((2,)),
+            pltpu.SemaphoreType.DMA((5,)),
             pltpu.SemaphoreType.DMA((chunks,)),
             pltpu.SemaphoreType.DMA((4, devices, parts)),
             pltpu.SemaphoreType.DMA((devices, parts)),
@@ -389,7 +433,7 @@
         compiler_params=pltpu.CompilerParams(
             collective_id=0, has_side_effects=True, vmem_limit_bytes=EXCHANGE_LIMIT
         ),
-    )(counts, snps, vectors, rider, scores)
+    )(*[pltpu.with_memory_space_constraint(operand, pltpu.HBM) for operand in operands])
 
 
 def per_device(eig_vectors, eig_values, eig_count, snp_count, zscores, samples):
@@ -400,6 +444,9 @@
     panel_index = slot_index // spacing
     group_index = slot_index % spacing
     blocks_here, snp_rows, panel_width = zscores.shape[1:]
+    if spacing == 1 and panels == 2 * ROUNDS and blocks_here == panels // 2:
+        raw, scale = exchange(eig_vectors, eig_values, samples, eig_count, snp_count, zscores)
+        return raw * scale[:, None, None]
     counts = lax.dynamic_slice_in_dim(eig_count, group_index * blocks_here, blocks_here)
     snps = lax.dynamic_slice_in_dim(snp_count, group_index * blocks_here, blocks_here)
     rounds = jnp.arange(ROUNDS + 1, dtype=jnp.int32)
@@ -407,10 +454,6 @@
     scales = samples.astype(jnp.float32).reshape(panels, panel_width)
     own_scale = lax.dynamic_index_in_dim(scales, panel_index, 0, keepdims=False)
     scale = 1.0 / jnp.sqrt(own_scale[None, :, None] * scales[partners][:, None, :])
-
-    if spacing == 1 and panels == 2 * ROUNDS and blocks_here == panels // 2:
-        raw = exchange(eig_vectors, eig_values, counts, snps, zscores)
-        return raw * scale[:, None, None]
     members = [[g + spacing * i for i in range(panels)] for g in range(spacing)]
     gather = functools.partial(
         lax.all_gather, axis_name="panel", axis_index_groups=members if spacing > 1 else None

time: 87.1 us -> 76.7 us (0.88)
  local copies, waits for them, and re-layouts: 5.18 us -> 0 us
  Pallas kernels: 78.1 us -> 73.1 us
    pallas_call x1, Pallas kernels: 78.1 us -> 73.1 us  [exchange(): pl.pallas_call(exchange_kernel, out_shape=[jax.ShapeDtypeStruct((rounds,...]
    unnamed x8 -> x0, local copies, waits for them, and re-layouts: 3.87 us -> none
where the time goes in v2:
time: 76.7 us; the launch traced here: 76.1 us
  Pallas kernels  73.1 us (95%)
  other arithmetic  3.02 us (4%)
    pallas_call x1, Pallas kernels, exchange(): pl.pallas_call(exchange_kernel, out_shape=[jax.ShapeDtypeStruct((rounds,...  73.1 us
    mul x1, other arithmetic, per_device(): return raw * scale[:, None, None]  3.02 us

profile of v2, /device:TPU:0, one launch (start us, length us, event | category | flops | bytes accessed | tf_op | source)
XLA Modules:
  0.0 76.1 jit_solution(7660337052929796834)
XLA Ops:
  0.0 73.1 %shard_map.64 = (f32[9,1,8,128,128]{4,3,2,1,0:T(8,128)S(1)}, f32[9,128,128]{2,1,0:T(8,128)S(1)}) custom-call(s32[8]{0:T(128)} %all_counts.1, s32[8]{0:T(128)} %all_snps.1, bf16[160,1024]{1,0:T(8,128)(2,1)} %own.1, bf16[160]{0:T(256)(128)(2,1)} %own_values.1, bf16[16,128]{1,0:T(8,128)(2,1)} %bitcast.1, bf16[1,8,1024,128]{3,2,1,0:T(8,128)(2,1)} %scores.1), custom_call_target="tpu_custom_call" | custom-call | tf_op jit(solution)/shard_map/pallas_call | solution.py:407
  73.1 3.0 %broadcast_multiply_fusion = f32[9,1,8,128,128]{4,3,2,1,0:T(8,128)} fusion(f32[9,1,8,128,128]{4,3,2,1,0:T(8,128)S(1)} %get-tuple-element.7, f32[9,128,128]{2,1,0:T(8,128)S(1)} %get-tuple-element.8), kind=kLoop, calls=%fused_computation | loop fusion | flops 1179648 | bytes 10027008 | tf_op jit(solution)/shard_map/mul | solution.py:449

commit v3 on v2

--- a/solution.py
+++ b/solution.py
@@ -98,7 +98,7 @@
 
 def exchange_kernel(all_counts, all_snps, own, own_values, samples, scores, out, scale, counts, snps,
                     flat_values, units, held, values, left, store, raw, masked, here, load,
-                    send1, recv1, send2, recv2):
+                    sent, recv1, recv2):
     line = lax.axis_size("panel") // 4
     me = lax.axis_index("panel")
     z = me // 4
@@ -178,7 +178,7 @@
         )
 
     def move1(source, part, way, target, first=False):
-        sems = send1.at[way, source, part], recv1.at[source, part]
+        sems = sent.at[0], recv1.at[source, part]
         if part == parts - 1:
             return remote(values.at[source], values.at[source], *sems, target)
         rows = pl.ds(source * piece + part * part_rows, part_rows)
@@ -190,7 +190,7 @@
 
     def move2(source, chunk, way, target):
         block = held.at[source, pl.ds(chunk * pair_rows, pair_rows)]
-        return remote(block, block, send2.at[way, source, chunk], recv2.at[source, chunk], target)
+        return remote(block, block, sent.at[1], recv2.at[source, chunk], target)
 
     def arrive2(source, chunk):
         move2(source, chunk, 0, beside).wait_recv()
@@ -425,9 +425,8 @@
             pltpu.VMEM((chunks, snp_rows, 2 * width), jnp.bfloat16),
             pltpu.SemaphoreType.DMA((5,)),
             pltpu.SemaphoreType.DMA((chunks,)),
-            pltpu.SemaphoreType.DMA((4, devices, parts)),
+            pltpu.SemaphoreType.DMA((2,)),
             pltpu.SemaphoreType.DMA((devices, parts)),
-            pltpu.SemaphoreType.DMA((4, devices, chunks)),
             pltpu.SemaphoreType.DMA((devices, chunks)),
         ],
         compiler_params=pltpu.CompilerParams(

time: 76.7 us -> 72.7 us (0.948)
  Pallas kernels: 73.1 us -> 69.1 us
    pallas_call x1, Pallas kernels: 73.1 us -> 69.1 us  [exchange(): pl.pallas_call(exchange_kernel, out_shape=[jax.ShapeDtypeStruct((rounds,...]
where the time goes in v3:
time: 72.7 us; the launch traced here: 72.1 us
  Pallas kernels  69.1 us (95%)
  other arithmetic  3.02 us (4%)
    pallas_call x1, Pallas kernels, exchange(): pl.pallas_call(exchange_kernel, out_shape=[jax.ShapeDtypeStruct((rounds,...  69.1 us
    mul x1, other arithmetic, per_device(): return raw * scale[:, None, None]  3.02 us

profile of v3, /device:TPU:0, one launch (start us, length us, event | category | flops | bytes accessed | tf_op | source)
XLA Modules:
  0.0 72.1 jit_solution(1806446506467688259)
XLA Ops:
  0.0 69.1 %shard_map.64 = (f32[9,1,8,128,128]{4,3,2,1,0:T(8,128)S(1)}, f32[9,128,128]{2,1,0:T(8,128)S(1)}) custom-call(s32[8]{0:T(128)} %all_counts.1, s32[8]{0:T(128)} %all_snps.1, bf16[160,1024]{1,0:T(8,128)(2,1)} %own.1, bf16[160]{0:T(256)(128)(2,1)} %own_values.1, bf16[16,128]{1,0:T(8,128)(2,1)} %bitcast.1, bf16[1,8,1024,128]{3,2,1,0:T(8,128)(2,1)} %scores.1), custom_call_target="tpu_custom_call" | custom-call | tf_op jit(solution)/shard_map/pallas_call | solution.py:407
  69.1 3.0 %broadcast_multiply_fusion = f32[9,1,8,128,128]{4,3,2,1,0:T(8,128)} fusion(f32[9,1,8,128,128]{4,3,2,1,0:T(8,128)S(1)} %get-tuple-element.7, f32[9,128,128]{2,1,0:T(8,128)S(1)} %get-tuple-element.8), kind=kLoop, calls=%fused_computation | loop fusion | flops 1179648 | bytes 10027008 | tf_op jit(solution)/shard_map/mul | solution.py:448

commit v4 on v3

--- a/solution.py
+++ b/solution.py
@@ -97,7 +97,7 @@
 
 
 def exchange_kernel(all_counts, all_snps, own, own_values, samples, scores, out, scale, counts, snps,
-                    flat_values, units, held, values, left, store, raw, masked, here, load,
+                    flat_values, units, held, values, left, store, raw, masked, here, load, shipped,
                     sent, recv1, recv2):
     line = lax.axis_size("panel") // 4
     me = lax.axis_index("panel")
@@ -113,7 +113,8 @@
     inner = (z > 0) & (z < top)
     edge = (z == 0) | (z == top)
     up, down, across, beside = me + 4, me - 4, me + 2 - 4 * y, me + 1 - 2 * k
-    skip = me + 8 - 16 * (z // 2)
+    inward = jnp.where(z == 0, up, down)
+    outward = jnp.where(z == 1, down, up)
     pending = []
 
     def order(plane, step):
@@ -146,7 +147,6 @@
 
     pl.when(z < top)(functools.partial(greet, up))
     pl.when(z > 0)(functools.partial(greet, down))
-    pl.when(z < 2)(functools.partial(greet, skip))
     for target in (across, beside):
         greet(target)
     for copy in local[1:]:
@@ -158,7 +158,7 @@
         ride.astype(jnp.bfloat16), hot.astype(jnp.bfloat16), preferred_element_type=jnp.float32
     )
     values[me] = ride[0:1]
-    pl.semaphore_wait(barrier, 2 + jnp.where(z > 0, 1, 0) + jnp.where(z < top, 1, 0) + z // 2)
+    pl.semaphore_wait(barrier, jnp.where(inner, 4, 3))
 
     def start(condition, copy):
         if condition is None:
@@ -198,39 +198,106 @@
     def both(a, b):
         return b if a is None else a & b
 
-    def column(step, condition=None):
+    def column(step, condition, some=None):
         plane = order(z, step)
         source = plane * 4 + y * 2 + k
-        for part in range(parts):
-            if condition is None:
-                arrive1(source, part)
+        for part in range(parts) if some is None else some:
+            wait(condition, arrive1, source, part)
+            if step < top or part == parts - 1:
+                start(condition & (plane < z) & (z < top), move1(source, part, 0, up))
+                held_back = (z == 2) if step == 1 and part > 0 else (z < 0)
+                start(condition & (plane > z) & (z > 0) & ~held_back, move1(source, part, 1, down))
+            if step == 1:
+                start(condition & edge, move1(source, part, 2, across))
             else:
-                pl.when(condition)(functools.partial(arrive1, source, part))
-            start(both(condition, (plane < z) & (z < top)), move1(source, part, 0, up))
-            start(both(condition, (plane > z) & (z > 0)), move1(source, part, 1, down))
-            start(condition, move1(source, part, 2, across))
+                start(condition, move1(source, part, 2, across))
             start(condition, move1(source, part, 3, beside))
 
-    def sideways(step):
+    def column_rest():
+        for part in range(1, parts):
+            start(z == 2, move1(me + 4, part, 1, down))
+
+    def passing(step, condition):
+        source, chunk = me + 4, order(z + 1, step)
+        wait(condition, arrive2, source, chunk)
+        start(condition, move2(source, chunk, 1, down))
+
+    def sideways(step, condition=None, some=None):
         source = order(z, step) * 4 + 2 - 2 * y + k
-        for part in range(parts):
-            arrive1(source, part)
-            start(None, move1(source, part, 3, beside))
+        for part in range(parts) if some is None else some:
+            wait(condition, arrive1, source, part)
+            start(condition, move1(source, part, 3, beside))
+            if step == 0:
+                start(both(condition, edge), move1(source, part, 0, inward))
 
     def mask(step):
         loads[step].wait()
         place_masked(snps, raw.at[pl.ds(2 * step, 2)], order(z, step), masked.at[step])
 
-    def finish(step):
+    def wait(condition, arrive, *where):
+        if condition is None:
+            arrive(*where)
+        else:
+            pl.when(condition)(functools.partial(arrive, *where))
+
+    def beside_pieces(step, condition, some):
         plane = order(z, step)
         for source in (plane * 4 + y * 2 + 1 - k, plane * 4 + 2 - 2 * y + 1 - k):
-            for part in range(parts):
-                arrive1(source, part)
+            for part in some:
+                wait(condition, arrive1, source, part)
+
+    def compute(step):
+        plane = order(z, step)
         rows = pl.ds(plane * pair_rows, pair_rows)
         held[me, rows] = project_rows(store[rows], masked[step], counts[2 * plane])
-        start(z < top, move2(me, plane, 0, up))
-        start(k == 0, move2(me, plane, 3, beside))
-        weigh(plane)
+
+    def finish(step, condition=None):
+        plane = order(z, step)
+        beside_pieces(step, condition, range(parts))
+        wait(condition, compute, step)
+        start(both(condition, z < top), move2(me, plane, 0, up))
+        start((z == 2) if step == top else (z >= 2), move2(me, plane, 1, down))
+        start(both(condition, k == 0), move2(me, plane, 3, beside))
+        wait(condition, weigh, plane)
+
+    def ship(half):
+        block = 2 * order(z, top) + half
+        return remote(
+            scores.at[0, pl.ds(block, 1)],
+            raw.at[pl.ds(2 * line + half, 1)],
+            sent.at[2],
+            shipped.at[half],
+            inward,
+        )
+
+    def compute_outside():
+        plane = order(z, top)
+        for half in range(2):
+            ship(half).wait_recv()
+        place_masked(snps, raw.at[pl.ds(2 * line, 2)], plane, masked.at[line])
+        rows = pl.ds(plane * pair_rows, pair_rows)
+        held[outward, rows] = project_rows(store[rows], masked[line], counts[2 * plane])
+
+    def outside():
+        plane = order(z, top)
+        pl.when(inner)(compute_outside)
+        start(inner, move2(outward, plane, 0, up))
+        start(inner & ~late_return, move2(outward, plane, 1, down))
+        start(z == 1, move2(outward, plane, 2, across))
+        start(z == 1, move2(outward, plane, 3, beside))
+
+    late_return = (z == 1) & (y == 1)
+
+    def outside_rest():
+        start(late_return, move2(outward, order(z, top), 1, down))
+
+    def returned(condition):
+        plane = order(z, top)
+        beside_pieces(top, condition, [parts - 1])
+        wait(condition, arrive2, me, plane)
+        start(condition & (k == 0), move2(me, plane, 3, beside))
+        start(condition & (y == 0), move2(me, plane, 2, across))
+        wait(condition, weigh, plane)
 
     def weigh(index):
         rows = pl.ds(index * pair_rows, pair_rows)
@@ -257,28 +324,21 @@
     def plane_behind(lag):
         return lax.rem(z - lag + line, line)
 
-    def own_across(step):
-        start(y == 0, move2(me, order(z, step), 2, across))
-
-    def far(step):
-        start(z >= 2, move2(me, order(z, step), 1, skip))
+    def own_across(step, condition=None):
+        start(both(condition, y == 0), move2(me, order(z, step), 2, across))
 
     def relay(step, turn, condition=None):
         lag = jnp.where(z == 0, 2 - turn, 1 + turn)
         plane = plane_behind(lag)
         source = plane * 4 + y * 2 + k
         chunk = order(plane, step)
-        if condition is None:
-            arrive2(source, chunk)
-        else:
-            pl.when(condition)(functools.partial(arrive2, source, chunk))
+        wait(condition, arrive2, source, chunk)
         start(both(condition, (lag == 1) & inner), move2(source, chunk, 0, up))
         start(both(condition, (lag == 2) & (z == 1)), move2(source, chunk, 1, down))
         start(both(condition, (lag == 1) | (y == 1)), move2(source, chunk, 2, across))
         start(both(condition, (lag == 1) | (k == 1)), move2(source, chunk, 3, beside))
 
     cross = [plane_behind(lag + 1 - y) * 4 + (1 - y) * 2 + k for lag in range(2)]
-    near = [plane_behind(lag) * 4 + y * 2 + k for lag in range(3)]
     swap = 1 - 2 * k
 
     def cross_over(step):
@@ -287,8 +347,18 @@
             arrive2(source, chunk)
             start(None, move2(source, chunk, 3, beside))
 
+    def turn_of(source, place):
+        plane = source // 4
+        late = sum(jnp.where(order(plane, step) == order(z, top), step, 0) for step in range(line))
+        if place == 2:
+            step = late
+        else:
+            rank = min(place, 2)
+            step = rank + jnp.where(rank >= late, 1, 0)
+        return order(plane, jnp.where(edge, step, place))
+
     def gram(source, step, number, own_panel=False):
-        chunk = order(source // 4, step)
+        chunk = turn_of(source, step)
         rows = pl.ds(chunk * pair_rows, pair_rows)
         both = jnp.dot(left[chunk], held[source, rows], preferred_element_type=jnp.float32)
         width = both.shape[1]
@@ -302,27 +372,35 @@
                 part = part - jnp.where(same, count, 0.0)
             out[number, 0, 2 * chunk + side] = part
 
-    def grams_near(step):
-        for lag, source in enumerate(near):
-            gram(source, step, 4 * lag, lag == 0)
-
-    def grams_near_beside(step):
-        for lag, source in enumerate(near):
-            number = 4 * lag - swap
+    def lag_of(turn):
+        return turn if turn == 0 else jnp.where(z == 0, 3 - turn, turn)
+
+    def near_gram(turn, *places):
+        lag = lag_of(turn)
+        for place in places:
+            gram(plane_behind(lag) * 4 + y * 2 + k, place, 4 * lag, turn == 0)
+
+    def near_beside(turn, *places):
+        lag = lag_of(turn)
+        number = 4 * lag - swap
+        source = plane_behind(lag) * 4 + y * 2 + 1 - k
+        for place in places:
 
             @pl.when((number >= 0) & (number < out.shape[0]))
             def _():
-                arrive2(source + swap, order(source // 4, step))
-                gram(source + swap, step, number)
-
-    def grams_cross(step):
-        for lag, source in enumerate(cross):
-            gram(source, step, 4 * lag + 2)
-
-    def grams_cross_beside(step):
-        for lag, source in enumerate(cross):
-            arrive2(source + swap, order(source // 4, step))
-            gram(source + swap, step, 4 * lag + 2 - swap)
+                arrive2(source, turn_of(source, place))
+                gram(source, place, number)
+
+    def cross_gram(*places):
+        for place in places:
+            for lag, source in enumerate(cross):
+                gram(source, place, 4 * lag + 2)
+
+    def cross_beside(*places):
+        for place in places:
+            for lag, source in enumerate(cross):
+                arrive2(source + swap, turn_of(source, place))
+                gram(source + swap, place, 4 * lag + 2 - swap)
 
     for part in range(parts):
         start(z < top, move1(me, part, 0, up, True))
@@ -335,57 +413,97 @@
     mask(2)
     mask(3)
     scales()
-    column(1)
+    column(1, inner)
+    for some in ([0], list(range(1, parts))):
+        column(1, edge, some)
+        sideways(0, edge, some)
     column(2, inner)
-    sideways(0)
+    sideways(0, inner)
     finish(0)
+    column_rest()
+    start(edge, ship(0))
     column(2, edge)
-    column(3, inner)
-    sideways(1)
+    column(3, inner, [0])
+    passing(0, z == 1)
+    sideways(1, z == 1)
+    column(3, inner, [1, 2])
+    sideways(1, z != 1)
     finish(1)
-    far(0)
-    far(1)
+    own_across(0)
+    passing(1, z == 1)
     relay(0, 0, inner)
-    column(3, edge)
-    own_across(0)
+    passing(0, z == 2)
     sideways(2)
     finish(2)
-    far(2)
-    relay(0, 1, inner)
+    start(edge, ship(1))
+    relay(1, 0, z == 2)
+    passing(1, z == 2)
     relay(0, 0, edge)
-    sideways(3)
-    finish(3)
-    far(3)
+    column(3, edge, [parts - 1])
+    sideways(3, inner)
+    relay(0, 1, z == 1)
+    finish(3, inner)
     own_across(1)
+    relay(0, 1, z == 2)
+    near_gram(0, 0, 1, 3)
+    relay(1, 0, edge)
+    passing(2, inner)
+    relay(1, 0, z == 1)
+    near_beside(0, 0, 1, 3)
     relay(0, 1, edge)
-    relay(1, 0)
-    grams_near(0)
-    relay(1, 1)
+    near_gram(1, 0)
+    relay(2, 0, z == 2)
+    relay(1, 1, z == 1)
+    relay(2, 0, z == 1)
+    relay(2, 0, edge)
+    near_gram(1, 1)
+    near_beside(1, 0)
+    passing(3, (z == 1) & (y == 1))
+    own_across(2)
+    outside()
+    relay(3, 0, z == 2)
+    near_beside(1, 1)
+    relay(1, 1, edge)
+    near_gram(2, 0)
+    relay(2, 1, z == 1)
+    relay(1, 1, z == 2)
+    near_beside(2, 0)
+    relay(3, 0, (z == 3) | ((z == 0) & (y == 1)))
     cross_over(0)
-    own_across(2)
-    grams_near_beside(0)
-    relay(2, 0)
-    grams_cross(0)
-    relay(2, 1)
+    sideways(3, edge, [parts - 1])
+    own_across(3, inner)
+    relay(3, 1, z == 1)
+    passing(3, (z == 1) & (y == 0))
+    outside_rest()
+    relay(2, 1, z == 2)
+    relay(3, 1, z == 2)
+    relay(2, 1, z == 3)
+    returned((z == 3) | ((z == 0) & (y == 0)))
     cross_over(1)
-    own_across(3)
-    grams_near(1)
-    grams_cross_beside(0)
-    relay(3, 0)
-    grams_near_beside(1)
-    grams_cross(1)
-    relay(3, 1)
+    cross_gram(0)
+    relay(2, 1, z == 0)
+    cross_beside(0)
+    near_gram(2, 1)
+    near_beside(2, 1)
+    relay(3, 1, edge)
+    near_gram(2, 3)
     cross_over(2)
-    grams_cross_beside(1)
-    grams_near(2)
-    grams_near_beside(2)
-    grams_cross(2)
-    grams_near(3)
-    grams_near_beside(3)
-    grams_cross_beside(2)
+    cross_gram(1)
+    cross_beside(1)
+    near_beside(2, 3)
+    relay(3, 0, (z == 0) & (y == 0))
+    near_gram(1, 3)
+    near_beside(1, 3)
+    returned((z == 0) & (y == 1))
+    near_gram(0, 2)
+    near_gram(1, 2)
+    near_gram(2, 2)
+    near_beside(1, 2)
+    near_beside(2, 2)
     cross_over(3)
-    grams_cross(3)
-    grams_cross_beside(3)
+    cross_gram(2, 3)
+    near_beside(0, 2)
+    cross_beside(2, 3)
     for condition, copy in pending:
         if condition is None:
             copy.wait_send()
@@ -421,11 +539,12 @@
             pltpu.VMEM((devices, 1, pair_rows), jnp.float32),
             pltpu.VMEM((chunks, 2 * width, pair_rows), jnp.bfloat16),
             pltpu.VMEM((row_total, depth), jnp.bfloat16),
-            pltpu.VMEM((blocks, snp_rows, width), jnp.bfloat16),
-            pltpu.VMEM((chunks, snp_rows, 2 * width), jnp.bfloat16),
+            pltpu.VMEM((blocks + 2, snp_rows, width), jnp.bfloat16),
+            pltpu.VMEM((chunks + 1, snp_rows, 2 * width), jnp.bfloat16),
             pltpu.SemaphoreType.DMA((5,)),
             pltpu.SemaphoreType.DMA((chunks,)),
             pltpu.SemaphoreType.DMA((2,)),
+            pltpu.SemaphoreType.DMA((3,)),
             pltpu.SemaphoreType.DMA((devices, parts)),
             pltpu.SemaphoreType.DMA((devices, chunks)),
         ],

time: 72.7 us -> 69.2 us (0.952)
  Pallas kernels: 69.1 us -> 66 us
    pallas_call x1, Pallas kernels: 69.1 us -> 66 us  [exchange(): pl.pallas_call(exchange_kernel, out_shape=[jax.ShapeDtypeStruct((rounds,...]
where the time goes in v4:
time: 69.2 us; the launch traced here: 69.1 us
  Pallas kernels  66 us (95%)
  other arithmetic  3.02 us (4%)
    pallas_call x1, Pallas kernels, exchange(): pl.pallas_call(exchange_kernel, out_shape=[jax.ShapeDtypeStruct((rounds,...  66 us
    mul x1, other arithmetic, per_device(): return raw * scale[:, None, None]  3.02 us

profile of v4, /device:TPU:0, one launch (start us, length us, event | category | flops | bytes accessed | tf_op | source)
XLA Modules:
  0.0 69.1 jit_solution(2271820155580199120)
XLA Ops:
  0.0 66.0 %shard_map.64 = (f32[9,1,8,128,128]{4,3,2,1,0:T(8,128)S(1)}, f32[9,128,128]{2,1,0:T(8,128)S(1)}) custom-call(s32[8]{0:T(128)} %all_counts.1, s32[8]{0:T(128)} %all_snps.1, bf16[160,1024]{1,0:T(8,128)(2,1)} %own.1, bf16[160]{0:T(256)(128)(2,1)} %own_values.1, bf16[16,128]{1,0:T(8,128)(2,1)} %bitcast.1, bf16[1,8,1024,128]{3,2,1,0:T(8,128)(2,1)} %scores.1), custom_call_target="tpu_custom_call" | custom-call | tf_op jit(solution)/shard_map/pallas_call | solution.py:525
  66.0 3.0 %broadcast_multiply_fusion = f32[9,1,8,128,128]{4,3,2,1,0:T(8,128)} fusion(f32[9,1,8,128,128]{4,3,2,1,0:T(8,128)S(1)} %get-tuple-element.7, f32[9,128,128]{2,1,0:T(8,128)S(1)} %get-tuple-element.8), kind=kLoop, calls=%fused_computation | loop fusion | flops 1179648 | bytes 10027008 | tf_op jit(solution)/shard_map/mul | solution.py:567

commit v5 on v4

--- a/solution.py
+++ b/solution.py
@@ -10,6 +10,7 @@
 ROUNDS = 8
 LIMIT = 56 * 1024 * 1024
 EXCHANGE_LIMIT = 36 * 1024 * 1024
+PUT_LIMIT = 1024 * 1024
 
 
 def place_masked(snps, scores, pair, store):
@@ -96,9 +97,9 @@
     )(counts, slots, weighted, panels, scale)
 
 
-def exchange_kernel(all_counts, all_snps, own, own_values, samples, scores, out, scale, counts, snps,
-                    flat_values, units, held, values, left, store, raw, masked, here, load, shipped,
-                    sent, recv1, recv2):
+def exchange_kernel(all_counts, all_snps, own, own_values, samples, scores, out, counts, snps,
+                    flat_values, units, scale, held, values, left, store, raw, masked, here, load, shipped,
+                    sent, recv1, recv2, recv3):
     line = lax.axis_size("panel") // 4
     me = lax.axis_index("panel")
     z = me // 4
@@ -116,6 +117,7 @@
     inward = jnp.where(z == 0, up, down)
     outward = jnp.where(z == 1, down, up)
     pending = []
+    pieces = []
 
     def order(plane, step):
         near = jnp.minimum(plane, top - plane)
@@ -160,12 +162,17 @@
     values[me] = ride[0:1]
     pl.semaphore_wait(barrier, jnp.where(inner, 4, 3))
 
-    def start(condition, copy):
+    def start(condition, copy, group=None):
         if condition is None:
             copy.start()
         else:
             pl.when(condition)(copy.start)
-        pending.append((condition, copy))
+        (pending if group is None else group).append((condition, copy))
+
+    def drain(group):
+        for condition, copy in group:
+            wait(condition, copy.wait_send)
+        group.clear()
 
     def remote(source, target, send, recv, device):
         return pltpu.make_async_remote_copy(
@@ -192,6 +199,30 @@
         block = held.at[source, pl.ds(chunk * pair_rows, pair_rows)]
         return remote(block, block, sent.at[1], recv2.at[source, chunk], target)
 
+    def half2(source, chunk, half, target):
+        rows = pl.ds(chunk * pair_rows + half * (pair_rows // 2), pair_rows // 2)
+        block = held.at[source, rows]
+        arrival = recv3.at[source] if half else recv2.at[source, chunk]
+        return remote(block, block, sent.at[1], arrival, target)
+
+    def give2(step, condition, source, chunk, target, some=range(2)):
+        if step < top:
+            start(condition, move2(source, chunk, 0, target))
+        else:
+            for half in some:
+                start(condition, half2(source, chunk, half, target))
+
+    def take2(step, condition, source, chunk, onward=()):
+        if step < top:
+            wait(condition, arrive2, source, chunk)
+            for where, target in onward:
+                give2(step, where, source, chunk, target)
+        else:
+            for half in range(2):
+                wait(condition, half2(source, chunk, half, beside).wait_recv)
+                for where, target in onward:
+                    give2(step, where, source, chunk, target, [half])
+
     def arrive2(source, chunk):
         move2(source, chunk, 0, beside).wait_recv()
 
@@ -204,31 +235,30 @@
         for part in range(parts) if some is None else some:
             wait(condition, arrive1, source, part)
             if step < top or part == parts - 1:
-                start(condition & (plane < z) & (z < top), move1(source, part, 0, up))
+                start(condition & (plane < z) & (z < top), move1(source, part, 0, up), pieces)
                 held_back = (z == 2) if step == 1 and part > 0 else (z < 0)
-                start(condition & (plane > z) & (z > 0) & ~held_back, move1(source, part, 1, down))
+                start(condition & (plane > z) & (z > 0) & ~held_back, move1(source, part, 1, down), pieces)
             if step == 1:
-                start(condition & edge, move1(source, part, 2, across))
+                start(condition & edge, move1(source, part, 2, across), pieces)
             else:
-                start(condition, move1(source, part, 2, across))
-            start(condition, move1(source, part, 3, beside))
+                start(condition, move1(source, part, 2, across), pieces)
+            start(condition, move1(source, part, 3, beside), pieces)
 
     def column_rest():
         for part in range(1, parts):
-            start(z == 2, move1(me + 4, part, 1, down))
+            start(z == 2, move1(me + 4, part, 1, down), pieces)
 
     def passing(step, condition):
-        source, chunk = me + 4, order(z + 1, step)
-        wait(condition, arrive2, source, chunk)
-        start(condition, move2(source, chunk, 1, down))
+        source = me + 4
+        take2(step, condition, source, order(z + 1, step), [(condition, down)])
 
     def sideways(step, condition=None, some=None):
         source = order(z, step) * 4 + 2 - 2 * y + k
         for part in range(parts) if some is None else some:
             wait(condition, arrive1, source, part)
-            start(condition, move1(source, part, 3, beside))
+            start(condition, move1(source, part, 3, beside), pieces)
             if step == 0:
-                start(both(condition, edge), move1(source, part, 0, inward))
+                start(both(condition, edge), move1(source, part, 0, inward), pieces)
 
     def mask(step):
         loads[step].wait()
@@ -255,8 +285,8 @@
         plane = order(z, step)
         beside_pieces(step, condition, range(parts))
         wait(condition, compute, step)
-        start(both(condition, z < top), move2(me, plane, 0, up))
-        start((z == 2) if step == top else (z >= 2), move2(me, plane, 1, down))
+        give2(step, both(condition, z < top), me, plane, up)
+        give2(step, (z == 2) if step == top else (z >= 2), me, plane, down)
         start(both(condition, k == 0), move2(me, plane, 3, beside))
         wait(condition, weigh, plane)
 
@@ -281,22 +311,22 @@
     def outside():
         plane = order(z, top)
         pl.when(inner)(compute_outside)
-        start(inner, move2(outward, plane, 0, up))
-        start(inner & ~late_return, move2(outward, plane, 1, down))
-        start(z == 1, move2(outward, plane, 2, across))
+        for half in range(2):
+            give2(top, inner, outward, plane, up, [half])
+            give2(top, inner & ~late_return, outward, plane, down, [half])
+            give2(top, z == 1, outward, plane, across, [half])
         start(z == 1, move2(outward, plane, 3, beside))
 
     late_return = (z == 1) & (y == 1)
 
     def outside_rest():
-        start(late_return, move2(outward, order(z, top), 1, down))
+        give2(top, late_return, outward, order(z, top), down)
 
     def returned(condition):
         plane = order(z, top)
         beside_pieces(top, condition, [parts - 1])
-        wait(condition, arrive2, me, plane)
+        take2(top, condition, me, plane, [(condition & (y == 0), across)])
         start(condition & (k == 0), move2(me, plane, 3, beside))
-        start(condition & (y == 0), move2(me, plane, 2, across))
         wait(condition, weigh, plane)
 
     def weigh(index):
@@ -325,17 +355,19 @@
         return lax.rem(z - lag + line, line)
 
     def own_across(step, condition=None):
-        start(both(condition, y == 0), move2(me, order(z, step), 2, across))
+        give2(step, both(condition, y == 0), me, order(z, step), across)
 
     def relay(step, turn, condition=None):
         lag = jnp.where(z == 0, 2 - turn, 1 + turn)
         plane = plane_behind(lag)
         source = plane * 4 + y * 2 + k
         chunk = order(plane, step)
-        wait(condition, arrive2, source, chunk)
-        start(both(condition, (lag == 1) & inner), move2(source, chunk, 0, up))
-        start(both(condition, (lag == 2) & (z == 1)), move2(source, chunk, 1, down))
-        start(both(condition, (lag == 1) | (y == 1)), move2(source, chunk, 2, across))
+        onward = [
+            (both(condition, (lag == 1) & inner), up),
+            (both(condition, (lag == 2) & (z == 1)), down),
+            (both(condition, (lag == 1) | (y == 1)), across),
+        ]
+        take2(step, condition, source, chunk, onward)
         start(both(condition, (lag == 1) | (k == 1)), move2(source, chunk, 3, beside))
 
     cross = [plane_behind(lag + 1 - y) * 4 + (1 - y) * 2 + k for lag in range(2)]
@@ -344,7 +376,7 @@
     def cross_over(step):
         for source in cross:
             chunk = order(source // 4, step)
-            arrive2(source, chunk)
+            take2(step, None, source, chunk)
             start(None, move2(source, chunk, 3, beside))
 
     def turn_of(source, place):
@@ -370,23 +402,24 @@
                 same = across_rows == lax.broadcasted_iota(jnp.int32, shape, 1)
                 count = counts[2 * chunk + side].astype(jnp.float32)
                 part = part - jnp.where(same, count, 0.0)
-            out[number, 0, 2 * chunk + side] = part
+            out[number, 0, 2 * chunk + side] = part * scale[number]
 
     def lag_of(turn):
         return turn if turn == 0 else jnp.where(z == 0, 3 - turn, turn)
 
-    def near_gram(turn, *places):
+    def near_gram(turn, *places, condition=None):
         lag = lag_of(turn)
+        source = plane_behind(lag) * 4 + y * 2 + k
         for place in places:
-            gram(plane_behind(lag) * 4 + y * 2 + k, place, 4 * lag, turn == 0)
-
-    def near_beside(turn, *places):
+            wait(condition, gram, source, place, 4 * lag, turn == 0)
+
+    def near_beside(turn, *places, condition=None):
         lag = lag_of(turn)
         number = 4 * lag - swap
         source = plane_behind(lag) * 4 + y * 2 + 1 - k
         for place in places:
 
-            @pl.when((number >= 0) & (number < out.shape[0]))
+            @pl.when(both(condition, (number >= 0) & (number < out.shape[0])))
             def _():
                 arrive2(source, turn_of(source, place))
                 gram(source, place, number)
@@ -403,25 +436,24 @@
                 gram(source + swap, place, 4 * lag + 2 - swap)
 
     for part in range(parts):
-        start(z < top, move1(me, part, 0, up, True))
-        start(z > 0, move1(me, part, 1, down, True))
-        start(None, move1(me, part, 2, across, True))
-        start(None, move1(me, part, 3, beside, True))
+        start(z < top, move1(me, part, 0, up, True), pieces)
+        start(z > 0, move1(me, part, 1, down, True), pieces)
+        start(None, move1(me, part, 2, across, True), pieces)
+        start(None, move1(me, part, 3, beside, True), pieces)
     mask(0)
     local[0].wait()
     mask(1)
     mask(2)
     mask(3)
     scales()
-    column(1, inner)
     for some in ([0], list(range(1, parts))):
+        column(1, inner, some)
+        column(2, inner, some)
         column(1, edge, some)
         sideways(0, edge, some)
-    column(2, inner)
     sideways(0, inner)
     finish(0)
     column_rest()
-    start(edge, ship(0))
     column(2, edge)
     column(3, inner, [0])
     passing(0, z == 1)
@@ -429,6 +461,7 @@
     column(3, inner, [1, 2])
     sideways(1, z != 1)
     finish(1)
+    start(edge, ship(0))
     own_across(0)
     passing(1, z == 1)
     relay(0, 0, inner)
@@ -436,8 +469,8 @@
     sideways(2)
     finish(2)
     start(edge, ship(1))
+    passing(1, z == 2)
     relay(1, 0, z == 2)
-    passing(1, z == 2)
     relay(0, 0, edge)
     column(3, edge, [parts - 1])
     sideways(3, inner)
@@ -487,6 +520,12 @@
     near_beside(2, 1)
     relay(3, 1, edge)
     near_gram(2, 3)
+    last_return = (z == 0) & (y == 1)
+    for turn in range(3):
+        near_gram(turn, 2, condition=~last_return)
+    for turn in range(3):
+        near_beside(turn, 2, condition=~last_return)
+    drain(pieces)
     cross_over(2)
     cross_gram(1)
     cross_beside(1)
@@ -494,21 +533,15 @@
     relay(3, 0, (z == 0) & (y == 0))
     near_gram(1, 3)
     near_beside(1, 3)
-    returned((z == 0) & (y == 1))
-    near_gram(0, 2)
-    near_gram(1, 2)
-    near_gram(2, 2)
-    near_beside(1, 2)
-    near_beside(2, 2)
+    returned(last_return)
+    for turn in range(3):
+        near_gram(turn, 2, condition=last_return)
+    for turn in range(3):
+        near_beside(turn, 2, condition=last_return)
     cross_over(3)
     cross_gram(2, 3)
-    near_beside(0, 2)
     cross_beside(2, 3)
-    for condition, copy in pending:
-        if condition is None:
-            copy.wait_send()
-        else:
-            pl.when(condition)(copy.wait_send)
+    drain(pending)
 
 
 def exchange(vectors, values, samples, counts, snps, scores):
@@ -524,17 +557,15 @@
     operands = [counts, snps, vectors, values, samples.reshape(devices, width), scores]
     return pl.pallas_call(
         exchange_kernel,
-        out_shape=[
-            jax.ShapeDtypeStruct((rounds, 1, blocks, width, width), jnp.float32),
-            jax.ShapeDtypeStruct((rounds, width, width), jnp.float32),
-        ],
+        out_shape=jax.ShapeDtypeStruct((rounds, 1, blocks, width, width), jnp.float32),
         in_specs=[hbm] * len(operands),
-        out_specs=[pl.BlockSpec(memory_space=pltpu.VMEM)] * 2,
+        out_specs=pl.BlockSpec(memory_space=pltpu.VMEM),
         scratch_shapes=[
             pltpu.SMEM((blocks,), jnp.int32),
             pltpu.SMEM((blocks,), jnp.int32),
             pltpu.VMEM((piece,), jnp.bfloat16),
             pltpu.VMEM((devices, width), jnp.bfloat16),
+            pltpu.VMEM((rounds, width, width), jnp.float32),
             pltpu.VMEM((devices, row_total, width), jnp.bfloat16),
             pltpu.VMEM((devices, 1, pair_rows), jnp.float32),
             pltpu.VMEM((chunks, 2 * width, pair_rows), jnp.bfloat16),
@@ -547,11 +578,34 @@
             pltpu.SemaphoreType.DMA((3,)),
             pltpu.SemaphoreType.DMA((devices, parts)),
             pltpu.SemaphoreType.DMA((devices, chunks)),
+            pltpu.SemaphoreType.DMA((devices,)),
         ],
         compiler_params=pltpu.CompilerParams(
             collective_id=0, has_side_effects=True, vmem_limit_bytes=EXCHANGE_LIMIT
         ),
     )(*[pltpu.with_memory_space_constraint(operand, pltpu.HBM) for operand in operands])
+
+
+def put_kernel(source, target, done):
+    copies = [
+        pltpu.make_async_copy(source.at[index], target.at[index], done.at[index])
+        for index in range(source.shape[0])
+    ]
+    for copy in copies:
+        copy.start()
+    for copy in copies:
+        copy.wait()
+
+
+def put_out(array):
+    return pl.pallas_call(
+        put_kernel,
+        out_shape=jax.ShapeDtypeStruct(array.shape, array.dtype),
+        in_specs=[pl.BlockSpec(memory_space=pl.ANY)],
+        out_specs=pl.BlockSpec(memory_space=pl.ANY),
+        scratch_shapes=[pltpu.SemaphoreType.DMA((array.shape[0],))],
+        compiler_params=pltpu.CompilerParams(vmem_limit_bytes=PUT_LIMIT),
+    )(array)
 
 
 def per_device(eig_vectors, eig_values, eig_count, snp_count, zscores, samples):
@@ -563,8 +617,9 @@
     group_index = slot_index % spacing
     blocks_here, snp_rows, panel_width = zscores.shape[1:]
     if spacing == 1 and panels == 2 * ROUNDS and blocks_here == panels // 2:
-        raw, scale = exchange(eig_vectors, eig_values, samples, eig_count, snp_count, zscores)
-        return raw * scale[:, None, None]
+        return put_out(
+            exchange(eig_vectors, eig_values, samples, eig_count, snp_count, zscores)
+        )
     counts = lax.dynamic_slice_in_dim(eig_count, group_index * blocks_here, blocks_here)
     snps = lax.dynamic_slice_in_dim(snp_count, group_index * blocks_here, blocks_here)
     rounds = jnp.arange(ROUNDS + 1, dtype=jnp.int32)

time: 69.2 us -> 66.3 us (0.958)
  other arithmetic: 3.02 us -> 0 us
    mul x1 -> x0, other arithmetic: 3.02 us -> none  [per_device(): return raw * scale[:, None, None]]
    pallas_call x1 -> x2, Pallas kernels: 66 us -> 66.2 us  [the longest x1 63.9 us: exchange(): pl.pallas_call(exchange_kernel, out_shape=jax.ShapeDtypeStruct((rounds, 1...]
where the time goes in v5:
time: 66.3 us; the launch traced here: 66.2 us
  Pallas kernels  66.2 us (100%)
    pallas_call x1, Pallas kernels, exchange(): pl.pallas_call(exchange_kernel, out_shape=jax.ShapeDtypeStruct((rounds, 1...  63.9 us
    pallas_call x1, Pallas kernels, put_out(): pl.pallas_call(put_kernel, out_shape=jax.ShapeDtypeStruct(array.shape, ar...  2.25 us

profile of v5, /device:TPU:0, one launch (start us, length us, event | category | flops | bytes accessed | tf_op | source)
XLA Modules:
  0.0 66.2 jit_solution(4538078519519588051)
XLA Ops:
  0.0 63.9 %shard_map.64.source = f32[9,1,8,128,128]{4,3,2,1,0:T(8,128)S(1)} custom-call(s32[8]{0:T(128)} %all_counts.1, s32[8]{0:T(128)} %all_snps.1, bf16[160,1024]{1,0:T(8,128)(2,1)} %own.1, bf16[160]{0:T(256)(128)(2,1)} %own_values.1, bf16[16,128]{1,0:T(8,128)(2,1)} %bitcast.1, bf16[1,8,1024,128]{3,2,1,0:T(8,128)(2,1)} %scores.1), custom_call_target="tpu_custom_call" | custom-call | tf_op jit(solution)/shard_map/pallas_call | solution.py:558
  63.9 2.3 %shard_map.65 = f32[9,1,8,128,128]{4,3,2,1,0:T(8,128)} custom-call(f32[9,1,8,128,128]{4,3,2,1,0:T(8,128)S(1)} %shard_map.64.source), custom_call_target="tpu_custom_call" | custom-call | tf_op jit(solution)/shard_map/pallas_call | solution.py:601

commit v6 on v5

--- a/solution.py
+++ b/solution.py
@@ -111,6 +111,7 @@
     part_rows = piece // (parts - 1)
     chunks = recv2.shape[1]
     top = line - 1
+    fine = top - 1
     inner = (z > 0) & (z < top)
     edge = (z == 0) | (z == top)
     up, down, across, beside = me + 4, me - 4, me + 2 - 4 * y, me + 1 - 2 * k
@@ -137,9 +138,6 @@
         pltpu.make_async_copy(all_snps, snps, here.at[3]),
         pltpu.make_async_copy(samples, units, here.at[4]),
     ]
-    for copy in local + loads:
-        copy.start()
-
     barrier = pltpu.get_barrier_semaphore()
 
     def greet(target):
@@ -151,15 +149,11 @@
     pl.when(z > 0)(functools.partial(greet, down))
     for target in (across, beside):
         greet(target)
-    for copy in local[1:]:
-        copy.wait()
+    for copy in local + loads:
+        copy.start()
     spot = lax.broadcasted_iota(jnp.int32, (piece, pair_rows), 1) - lax.rem(me, 4) * piece
     hot = jnp.where(spot == lax.broadcasted_iota(jnp.int32, spot.shape, 0), 1.0, 0.0)
-    ride = jnp.broadcast_to(flat_values[...].astype(jnp.float32).reshape(1, piece), (8, piece))
-    ride = jnp.dot(
-        ride.astype(jnp.bfloat16), hot.astype(jnp.bfloat16), preferred_element_type=jnp.float32
-    )
-    values[me] = ride[0:1]
+    hot = hot.astype(jnp.bfloat16)
     pl.semaphore_wait(barrier, jnp.where(inner, 4, 3))
 
     def start(condition, copy, group=None):
@@ -195,36 +189,40 @@
     def arrive1(source, part):
         move1(source, part, 0, beside).wait_recv()
 
-    def move2(source, chunk, way, target):
+    def slot(source, target):
+        return jnp.minimum(lax.rem(target - source + 4 * line, 4 * line), recv2.shape[0] - 1)
+
+    def move2(source, chunk, way, target, sends=1):
         block = held.at[source, pl.ds(chunk * pair_rows, pair_rows)]
-        return remote(block, block, sent.at[1], recv2.at[source, chunk], target)
-
-    def half2(source, chunk, half, target):
+        return remote(block, block, sent.at[sends], recv2.at[slot(source, target), chunk], target)
+
+    def half2(step, source, chunk, half, target):
         rows = pl.ds(chunk * pair_rows + half * (pair_rows // 2), pair_rows // 2)
         block = held.at[source, rows]
-        arrival = recv3.at[source] if half else recv2.at[source, chunk]
+        place = slot(source, target)
+        arrival = recv3.at[place, step - fine] if half else recv2.at[place, chunk]
         return remote(block, block, sent.at[1], arrival, target)
 
     def give2(step, condition, source, chunk, target, some=range(2)):
-        if step < top:
-            start(condition, move2(source, chunk, 0, target))
+        if step < fine:
+            start(condition, move2(source, chunk, 0, target, 3), pieces)
         else:
             for half in some:
-                start(condition, half2(source, chunk, half, target))
+                start(condition, half2(step, source, chunk, half, target))
 
     def take2(step, condition, source, chunk, onward=()):
-        if step < top:
+        if step < fine:
             wait(condition, arrive2, source, chunk)
             for where, target in onward:
                 give2(step, where, source, chunk, target)
         else:
             for half in range(2):
-                wait(condition, half2(source, chunk, half, beside).wait_recv)
+                wait(condition, half2(step, source, chunk, half, me).wait_recv)
                 for where, target in onward:
                     give2(step, where, source, chunk, target, [half])
 
     def arrive2(source, chunk):
-        move2(source, chunk, 0, beside).wait_recv()
+        move2(source, chunk, 0, me).wait_recv()
 
     def both(a, b):
         return b if a is None else a & b
@@ -424,18 +422,27 @@
                 arrive2(source, turn_of(source, place))
                 gram(source, place, number)
 
-    def cross_gram(*places):
+    def cross_gram(*places, condition=None):
         for place in places:
             for lag, source in enumerate(cross):
-                gram(source, place, 4 * lag + 2)
-
-    def cross_beside(*places):
+                wait(condition, gram, source, place, 4 * lag + 2)
+
+    def cross_beside(*places, condition=None):
+        def beside_gram(source, place, number):
+            arrive2(source, turn_of(source, place))
+            gram(source, place, number)
+
         for place in places:
             for lag, source in enumerate(cross):
-                arrive2(source + swap, turn_of(source, place))
-                gram(source + swap, place, 4 * lag + 2 - swap)
+                wait(condition, beside_gram, source + swap, place, 4 * lag + 2 - swap)
 
     for part in range(parts):
+        if part == parts - 1:
+            for copy in local[1:]:
+                copy.wait()
+            ride = flat_values[...].astype(jnp.float32).reshape(1, piece)
+            ride = jnp.broadcast_to(ride, (8, piece)).astype(jnp.bfloat16)
+            values[me] = jnp.dot(ride, hot, preferred_element_type=jnp.float32)[0:1]
         start(z < top, move1(me, part, 0, up, True), pieces)
         start(z > 0, move1(me, part, 1, down, True), pieces)
         start(None, move1(me, part, 2, across, True), pieces)
@@ -528,19 +535,23 @@
     drain(pieces)
     cross_over(2)
     cross_gram(1)
-    cross_beside(1)
     near_beside(2, 3)
     relay(3, 0, (z == 0) & (y == 0))
     near_gram(1, 3)
-    near_beside(1, 3)
+    cross_beside(1)
     returned(last_return)
     for turn in range(3):
         near_gram(turn, 2, condition=last_return)
     for turn in range(3):
         near_beside(turn, 2, condition=last_return)
+    early = inner | ((z == 0) & (y == 0))
+    cross_gram(2, condition=early)
     cross_over(3)
-    cross_gram(2, 3)
-    cross_beside(2, 3)
+    cross_gram(2, condition=~early)
+    cross_beside(2)
+    cross_gram(3)
+    near_beside(1, 3)
+    cross_beside(3)
     drain(pending)
 
 
@@ -575,10 +586,10 @@
             pltpu.SemaphoreType.DMA((5,)),
             pltpu.SemaphoreType.DMA((chunks,)),
             pltpu.SemaphoreType.DMA((2,)),
-            pltpu.SemaphoreType.DMA((3,)),
+            pltpu.SemaphoreType.DMA((4,)),
             pltpu.SemaphoreType.DMA((devices, parts)),
-            pltpu.SemaphoreType.DMA((devices, chunks)),
-            pltpu.SemaphoreType.DMA((devices,)),
+            pltpu.SemaphoreType.DMA((rounds + 1, chunks)),
+            pltpu.SemaphoreType.DMA((rounds + 1, 2)),
         ],
         compiler_params=pltpu.CompilerParams(
             collective_id=0, has_side_effects=True, vmem_limit_bytes=EXCHANGE_LIMIT
@@ -588,8 +599,10 @@
 
 def put_kernel(source, target, done):
     copies = [
-        pltpu.make_async_copy(source.at[index], target.at[index], done.at[index])
-        for index in range(source.shape[0])
+        pltpu.make_async_copy(
+            source.at[pl.ds(index, 3)], target.at[pl.ds(index, 3)], done.at[index]
+        )
+        for index in range(0, source.shape[0], 3)
     ]
     for copy in copies:
         copy.start()

time: 66.3 us -> 65.9 us (level)
  no operation moved by 1% of the time
where the time goes in v6:
time: 65.9 us; the launch traced here: 65.7 us
  Pallas kernels  65.7 us (100%)
    pallas_call x1, Pallas kernels, exchange(): pl.pallas_call(exchange_kernel, out_shape=jax.ShapeDtypeStruct((rounds, 1...  63.5 us
    pallas_call x1, Pallas kernels, put_out(): pl.pallas_call(put_kernel, out_shape=jax.ShapeDtypeStruct(array.shape, ar...  2.26 us

profile of v6, /device:TPU:0, one launch (start us, length us, event | category | flops | bytes accessed | tf_op | source)
XLA Modules:
  0.0 65.7 jit_solution(8587528893572829091)
XLA Ops:
  0.0 63.5 %shard_map.64.source = f32[9,1,8,128,128]{4,3,2,1,0:T(8,128)S(1)} custom-call(s32[8]{0:T(128)} %all_counts.1, s32[8]{0:T(128)} %all_snps.1, bf16[160,1024]{1,0:T(8,128)(2,1)} %own.1, bf16[160]{0:T(256)(128)(2,1)} %own_values.1, bf16[16,128]{1,0:T(8,128)(2,1)} %bitcast.1, bf16[1,8,1024,128]{3,2,1,0:T(8,128)(2,1)} %scores.1), custom_call_target="tpu_custom_call" | custom-call | tf_op jit(solution)/shard_map/pallas_call | solution.py:569
  63.5 2.3 %shard_map.65 = f32[9,1,8,128,128]{4,3,2,1,0:T(8,128)} custom-call(f32[9,1,8,128,128]{4,3,2,1,0:T(8,128)S(1)} %shard_map.64.source), custom_call_target="tpu_custom_call" | custom-call | tf_op jit(solution)/shard_map/pallas_call | solution.py:614

commit v7 on v6

--- a/solution.py
+++ b/solution.py
@@ -99,7 +99,7 @@
 
 def exchange_kernel(all_counts, all_snps, own, own_values, samples, scores, out, counts, snps,
                     flat_values, units, scale, held, values, left, store, raw, masked, here, load, shipped,
-                    sent, recv1, recv2, recv3):
+                    sent, recv1, recv4, recv2, recv3):
     line = lax.axis_size("panel") // 4
     me = lax.axis_index("panel")
     z = me // 4
@@ -111,7 +111,7 @@
     part_rows = piece // (parts - 1)
     chunks = recv2.shape[1]
     top = line - 1
-    fine = top - 1
+    fine = top
     inner = (z > 0) & (z < top)
     edge = (z == 0) | (z == top)
     up, down, across, beside = me + 4, me - 4, me + 2 - 4 * y, me + 1 - 2 * k
@@ -179,7 +179,10 @@
         )
 
     def move1(source, part, way, target, first=False):
-        sems = sent.at[0], recv1.at[source, part]
+        arrival = recv1.at[source // 2, part]
+        if way == 3:
+            arrival = recv4.at[source // 2, part // (parts - 1)]
+        sems = sent.at[0], arrival
         if part == parts - 1:
             return remote(values.at[source], values.at[source], *sems, target)
         rows = pl.ds(source * piece + part * part_rows, part_rows)
@@ -187,7 +190,13 @@
         return remote(origin, store.at[rows], *sems, target)
 
     def arrive1(source, part):
-        move1(source, part, 0, beside).wait_recv()
+        move1(source, part, 0, me).wait_recv()
+
+    def arrive_beside(source, some):
+        if len(some) > 1:
+            rows = store.at[pl.ds(source * piece, piece)]
+            remote(rows, rows, sent.at[0], recv4.at[source // 2, 0], me).wait_recv()
+        move1(source, parts - 1, 3, me).wait_recv()
 
     def slot(source, target):
         return jnp.minimum(lax.rem(target - source + 4 * line, 4 * line), recv2.shape[0] - 1)
@@ -271,8 +280,7 @@
     def beside_pieces(step, condition, some):
         plane = order(z, step)
         for source in (plane * 4 + y * 2 + 1 - k, plane * 4 + 2 - 2 * y + 1 - k):
-            for part in some:
-                wait(condition, arrive1, source, part)
+            wait(condition, arrive_beside, source, some)
 
     def compute(step):
         plane = order(z, step)
@@ -587,9 +595,10 @@
             pltpu.SemaphoreType.DMA((chunks,)),
             pltpu.SemaphoreType.DMA((2,)),
             pltpu.SemaphoreType.DMA((4,)),
-            pltpu.SemaphoreType.DMA((devices, parts)),
+            pltpu.SemaphoreType.DMA((devices // 2, parts)),
+            pltpu.SemaphoreType.DMA((devices // 2, 2)),
             pltpu.SemaphoreType.DMA((rounds + 1, chunks)),
-            pltpu.SemaphoreType.DMA((rounds + 1, 2)),
+            pltpu.SemaphoreType.DMA((rounds + 1, 1)),
         ],
         compiler_params=pltpu.CompilerParams(
             collective_id=0, has_side_effects=True, vmem_limit_bytes=EXCHANGE_LIMIT

time: 65.9 us -> 65.7 us (level)
  no operation moved by 1% of the time
where the time goes in v7:
time: 65.7 us; the launch traced here: 65.5 us
  Pallas kernels  65.5 us (100%)
    pallas_call x1, Pallas kernels, exchange(): pl.pallas_call(exchange_kernel, out_shape=jax.ShapeDtypeStruct((rounds, 1...  63.2 us
    pallas_call x1, Pallas kernels, put_out(): pl.pallas_call(put_kernel, out_shape=jax.ShapeDtypeStruct(array.shape, ar...  2.26 us

profile of v7, /device:TPU:0, one launch (start us, length us, event | category | flops | bytes accessed | tf_op | source)
XLA Modules:
  0.0 65.5 jit_solution(4134369553551034418)
XLA Ops:
  0.0 63.2 %shard_map.64.source = f32[9,1,8,128,128]{4,3,2,1,0:T(8,128)S(1)} custom-call(s32[8]{0:T(128)} %all_counts.1, s32[8]{0:T(128)} %all_snps.1, bf16[160,1024]{1,0:T(8,128)(2,1)} %own.1, bf16[160]{0:T(256)(128)(2,1)} %own_values.1, bf16[16,128]{1,0:T(8,128)(2,1)} %bitcast.1, bf16[1,8,1024,128]{3,2,1,0:T(8,128)(2,1)} %scores.1), custom_call_target="tpu_custom_call" | custom-call | tf_op jit(solution)/shard_map/pallas_call | solution.py:577
  63.3 2.3 %shard_map.65 = f32[9,1,8,128,128]{4,3,2,1,0:T(8,128)} custom-call(f32[9,1,8,128,128]{4,3,2,1,0:T(8,128)S(1)} %shard_map.64.source), custom_call_target="tpu_custom_call" | custom-call | tf_op jit(solution)/shard_map/pallas_call | solution.py:623
